TPU v7x, 512 devices: a whole 4x8x8 slice. The times are simulated.
512 devices in a mesh: dp: 64 (over y, z), fsdp: 8 (over x, core).
Axes of the slice: x: 4, y: 8, z: 8, core: 2. Of those that a mesh axis runs over, the one named last changes fastest.
Arguments:
- frames: bfloat16 [524288, 512], P(('dp', 'fsdp')), may hold values from -6 to 6
- utt_pairs: int32 [8, 64, 4], P('fsdp'), may hold values from 32 to 256, as said below
- utt_dest: int32 [8, 64, 4], P('fsdp'), may hold values from 0 to 63, as said below
- conv_weight: bfloat16 [1536, 512], P('dp'), may hold values from -0.15625 to 0.15625
- proj_weight: bfloat16 [512, 1536], P('dp'), may hold values from -0.25 to 0.25
- point_weight: bfloat16 [2, 1536, 1536], P(None, None, 'fsdp'), may hold values from -0.15625 to 0.15625
- depth_weight: float32 [31, 1536], replicated, may hold values from -1 to 1
- gain_first: float32 [1536], replicated, may hold values from 0.5 to 1.5
- gain_second: float32 [1536], replicated, may hold values from 0.5 to 1.5
Outputs:
- encoded: bfloat16 [262144, 1536], P(('dp', 'fsdp'))
Inputs may be any that keep to these rules, and one draw needn't show every extreme that they name: `utt_pairs`: every loader holds exactly 512 pairs and every sequence device receives exactly 512 pairs, from 4 different loaders. Each loader holds one utterance of exactly 256 pairs and one of exactly 32 pairs. `utt_dest`: the 4 utterances of loader i go to the 4 different sequence devices (i + k * 64 / 4) mod 64, k = 0 .. 3, in some order.
All inputs are finite; a program needn't handle non-finite values.
Results may differ from a plain program's by a relative error of at most 0.012.
Values may be sent and summed in bfloat16 or wider, within the bound.
No kernel may reach another device: no remote copies, remote signals or barrier semaphores. Data moves between devices by JAX's collectives and lax.ppermute only.
A program may use at most 64 MiB of HBM per device.

v0:
```python
import jax
import jax.numpy as jnp
from jax import lax
from jax.sharding import PartitionSpec as P


def passed_along(value, axis, steps):
    count = lax.axis_size(axis)
    pairs = [(source, (source + steps) % count) for source in range(count)]
    return lax.ppermute(value, axis, pairs)


def frontend(pair_rows, first_rows, conv_full):
    channels = pair_rows.shape[1] // 2
    even_frames = pair_rows[:, :channels]
    odd_frames = pair_rows[:, channels:]
    earlier = jnp.pad(odd_frames[:-1], ((1, 0), (0, 0)))
    earlier = jnp.where(first_rows[:, None], jnp.zeros_like(earlier), earlier)
    summed = jnp.dot(earlier, conv_full[:channels], preferred_element_type=jnp.float32)
    summed = summed + jnp.dot(
        even_frames, conv_full[channels : 2 * channels], preferred_element_type=jnp.float32
    )
    summed = summed + jnp.dot(
        odd_frames, conv_full[2 * channels :], preferred_element_type=jnp.float32
    )
    return jax.nn.relu(summed).astype(jnp.bfloat16)


def layer_norm(values, scales):
    centered = values - jnp.mean(values, axis=-1, keepdims=True)
    variance = jnp.mean(centered * centered, axis=-1, keepdims=True)
    return centered * lax.rsqrt(variance + 1e-05) * scales


def depthwise(gated, depth_weight, positions, lengths):
    row_count = gated.shape[0]
    kernel_size = depth_weight.shape[0]
    half_width = kernel_size // 2
    padded = jnp.pad(gated.astype(jnp.float32), ((half_width, half_width), (0, 0)))
    mixed = jnp.zeros(gated.shape, jnp.float32)
    for tap_index in range(kernel_size):
        offset = tap_index - half_width
        inside = (positions + offset >= 0) & (positions + offset < lengths)
        term = padded[tap_index : tap_index + row_count] * depth_weight[tap_index][None, :]
        mixed = mixed + jnp.where(inside[:, None], term, jnp.zeros_like(term))
    return mixed


def gate_product(normed, value_weight, gate_weight):
    value_part = jnp.dot(normed, value_weight, preferred_element_type=jnp.float32)
    gate_part = jnp.dot(normed, gate_weight, preferred_element_type=jnp.float32)
    return (value_part * jax.nn.sigmoid(gate_part)).astype(jnp.bfloat16)


def cut_pieces(source_rows, own_starts, slot_size, utt_count):
    padded = jnp.pad(source_rows, ((0, slot_size), (0, 0)))
    pieces = []
    for slot_index in range(utt_count):
        pieces.append(lax.dynamic_slice_in_dim(padded, own_starts[slot_index], slot_size, 0))
    return pieces


def body(
    frames,
    utt_pairs,
    utt_dest,
    conv_weight,
    proj_weight,
    point_weight,
    depth_weight,
    gain_first,
    gain_second,
):
    node_count = lax.axis_size("dp")
    own_index = lax.axis_index("dp")
    pair_count = frames.shape[0] // 2
    channels = frames.shape[1]
    utt_count = utt_pairs.shape[2]
    spacing = node_count // utt_count
    slot_size = pair_count // 2
    pair_table = utt_pairs[0]
    dest_table = utt_dest[0]
    loader_ids = jnp.arange(node_count, dtype=jnp.int32)
    slot_ids = jnp.arange(utt_count, dtype=jnp.int32)
    slot_table = (dest_table - loader_ids[:, None]) % node_count // spacing
    matches = (slot_table[:, :, None] == slot_ids[None, None, :]).astype(jnp.int32)
    loader_offsets = jnp.cumsum(pair_table, axis=1) - pair_table
    slot_counts = jnp.sum(matches * pair_table[:, :, None], axis=1)
    slot_starts = jnp.sum(matches * loader_offsets[:, :, None], axis=1)
    conv_full, proj_full = (
        lax.all_gather(conv_weight, "dp", axis=0, tiled=True),
        lax.all_gather(proj_weight, "dp", axis=0, tiled=True),
    )
    own_starts = slot_starts[own_index]
    sources = (own_index - slot_ids * spacing) % node_count
    piece_lengths = slot_counts[sources, slot_ids]
    earlier_pieces = (sources[None, :] < sources[:, None]).astype(jnp.int32)
    piece_offsets = jnp.sum(earlier_pieces * piece_lengths[None, :], axis=1)
    pair_rows = jnp.arange(pair_count, dtype=jnp.int32)
    inside = (
        (pair_rows[:, None] >= piece_offsets[None, :])
        & (pair_rows[:, None] < piece_offsets[None, :] + piece_lengths[None, :])
    ).astype(jnp.int32)
    piece_index = jnp.sum(inside * slot_ids[None, :], axis=1)
    positions = pair_rows - jnp.sum(inside * piece_offsets[None, :], axis=1)
    lengths = jnp.sum(inside * piece_lengths[None, :], axis=1)
    flat_slot = piece_index * slot_size + positions
    frame_pairs = frames.reshape(pair_count, 2 * channels)
    pieces = cut_pieces(frame_pairs, own_starts, slot_size, utt_count)
    arrived = [pieces[0]]
    for slot_index in range(1, utt_count):
        arrived.append(passed_along(pieces[slot_index], "dp", slot_index * spacing))
    stacked = jnp.concatenate(arrived, axis=0)
    packed = jnp.take(stacked, flat_slot, axis=0)
    front = frontend(packed, positions == 0, conv_full)
    projected = jnp.dot(front, proj_full, preferred_element_type=jnp.float32).astype(jnp.bfloat16)
    normed = layer_norm(projected.astype(jnp.float32), gain_first).astype(jnp.bfloat16)
    weight_part = lax.all_gather(point_weight, "fsdp", axis=2, tiled=True)
    gated = gate_product(normed, weight_part[0], weight_part[1])
    mixed = depthwise(gated, depth_weight, positions, lengths)
    scaled = layer_norm(mixed, gain_second)
    return (scaled * jax.nn.sigmoid(scaled)).astype(jnp.bfloat16)


def solution(mesh):
    in_specs = (
        P(("dp", "fsdp"), None),
        P("fsdp", None, None),
        P("fsdp", None, None),
        P("dp", None),
        P("dp", None),
        P(None, None, "fsdp"),
        P(),
        P(),
        P(),
    )
    out_specs = P(("dp", "fsdp"), None)
    return jax.shard_map(body, mesh=mesh, in_specs=in_specs, out_specs=out_specs, check_vma=False)
```

profile of v0, /device:TPU:1, one launch (start us, length us, event | category | flops | bytes accessed | tf_op | source)
XLA Modules:
  0.0 303.4 jit_solution(6321874885541037050)
XLA Ops:
  6.5 0.0 all-gather.4.cloned.1.call-start
  6.5 0.7 all-gather.4.cloned.1.call-update
  7.3 0.0 all-gather.6.cloned.1.call-start
  7.3 0.7 all-gather.6.cloned.1.call-update
  8.0 0.0 all-gather.8.cloned.1.call-start
  8.1 0.7 all-gather.8.cloned.1.call-update
  8.7 0.0 copy-start.1
  8.8 0.8 reduce_window_sum.11
  9.5 0.7 add_select_fusion
  10.2 0.7 select_reduce_fusion.4
  10.9 0.1 constant_dynamic-slice_fusion
  11.0 0.6 fusion.84
  16.7 1.4 reshape.518
  20.7 1.6 pad_dynamic-slice_fusion.3
  22.2 5.1 %collective-permute-start = (bf16[256,1024]{1,0:T(8,128)(2,1)S(1)}, bf16[256,1024]{1,0:T(8,128)(2,1)S(1)}, u32[]{:S(2)}, u32[]{:S(2)}) collective-permute-start(bf16[256,1024]{1,0:T(8,128)(2,1)S(1)} %get-tuple-element.44), channel_id=1, source_target_pairs={{0,128},{8,136},{16,144},{24,152},{32,160},{40,168},{48,176},{56,1... | collective-permute-start | bytes 1572872 | tf_op jit(solution)/shard_map/ppermute | solution.py:10
  27.3 5.7 %collective-permute-start.1 = (bf16[256,1024]{1,0:T(8,128)(2,1)S(1)}, bf16[256,1024]{1,0:T(8,128)(2,1)}, u32[]{:S(2)}, u32[]{:S(2)}) collective-permute-start(bf16[256,1024]{1,0:T(8,128)(2,1)S(1)} %get-tuple-element.45), channel_id=1, source_target_pairs={{0,256},{8,264},{16,272},{24,280},{32,288},{40,296},{48,304},{56,3... | collective-permute-start | bytes 1572872 | tf_op jit(solution)/shard_map/ppermute | solution.py:10
  33.0 5.0 %collective-permute-start.2 = (bf16[256,1024]{1,0:T(8,128)(2,1)S(1)}, bf16[256,1024]{1,0:T(8,128)(2,1)}, u32[]{:S(2)}, u32[]{:S(2)}) collective-permute-start(bf16[256,1024]{1,0:T(8,128)(2,1)S(1)} %get-tuple-element.46), channel_id=1, source_target_pairs={{0,384},{8,392},{16,400},{24,408},{32,416},{40,424},{48,432},{56,4... | collective-permute-start | bytes 1572872 | tf_op jit(solution)/shard_map/ppermute | solution.py:10
  38.0 0.6 gather_fusion
  38.6 0.2 select_reduce_fusion.5
  38.8 0.1 select_reduce_fusion.2
  38.9 0.0 copy-done.1
  39.0 0.8 slice_reduce_fusion.29
  39.8 0.3 slice_reduce_fusion.30
  40.1 0.1 compare_and_fusion.31
  40.2 1.1 collective-permute-done
  41.2 0.0 copy-start
  41.2 27.6 %collective-permute-done.1 = bf16[256,1024]{1,0:T(8,128)(2,1)} collective-permute-done((bf16[256,1024]{1,0:T(8,128)(2,1)S(1)}, bf16[256,1024]{1,0:T(8,128)(2,1)}, u32[]{:S(2)}, u32[]{:S(2)}) %collective-permute-start.1) | collective-permute-done | bytes 524320 | tf_op jit(solution)/shard_map/ppermute | solution.py:10
  68.8 11.9 %collective-permute-done.2 = bf16[256,1024]{1,0:T(8,128)(2,1)} collective-permute-done((bf16[256,1024]{1,0:T(8,128)(2,1)S(1)}, bf16[256,1024]{1,0:T(8,128)(2,1)}, u32[]{:S(2)}, u32[]{:S(2)}) %collective-permute-start.2) | collective-permute-done | bytes 524320 | tf_op jit(solution)/shard_map/ppermute | solution.py:10
  80.7 0.0 copy-done
  80.7 1.5 pad_maximum_fusion
  82.3 2.2 gather_fusion.1
  84.5 0.2 broadcast_select_fusion
  84.7 31.2 %all-gather.4.cloned.1.call-done = bf16[1536,512]{1,0:T(8,128)(2,1)} async-done(((bf16[24,512]{1,0:T(8,128)(2,1)}), bf16[1536,512]{1,0:T(8,128)(2,1)}) %all-gather.4.cloned.1.call-update) | async-done | bytes 1572880 | tf_op jit(solution)/shard_map/all_gather | solution.py:91
  116.0 1.5 fusion.62
  117.5 2.5 convolution_add_fusion.1
  120.0 0.0 copy-start.10
  120.0 78.9 %all-gather.6.cloned.1.call-done = bf16[512,1536]{1,0:T(8,128)(2,1)} async-done(((bf16[8,1536]{1,0:T(8,128)(2,1)}), bf16[512,1536]{1,0:T(8,128)(2,1)}) %all-gather.6.cloned.1.call-update) | async-done | bytes 1572880 | tf_op jit(solution)/shard_map/all_gather | solution.py:92
  198.9 3.2 %convert_reduce_fusion = (f32[512]{0:T(512)S(1)}, bf16[512,1536]{1,0:T(8,128)(2,1)S(1)}) fusion(bf16[512,1536]{1,0:T(8,128)(2,1)} %all-gather.6.cloned.1.call-done, f32[512,512]{1,0:T(8,128)} %convolution_add_fusion.1, bf16[1536,512]{1,0:T(8,128)(2,1)} %all-gather.4.cloned.1.call-done, bf16[512,1024]{1,0:T(8,128)(2,1)S(1)} %broadcast_select_fusion), kind=kOutput, calls=%fused_computation.7 | convolution fusion | flops 1076887040 | bytes 5244928 | tf_op jit(solution)/shard_map/dot_general | solution.py:116
  202.1 0.6 fusion.8
  202.7 59.3 %all-gather.8.cloned.1.call-done = bf16[2,1536,1536]{1,2,0:T(8,128)(2,1)} async-done(((bf16[2,1536,192]{1,2,0:T(8,128)(2,1)}), bf16[2,1536,1536]{1,2,0:T(8,128)(2,1)}) %all-gather.8.cloned.1.call-update) | async-done | bytes 9437200 | tf_op jit(solution)/shard_map/all_gather | solution.py:118
  261.9 0.0 copy-done.10
  261.9 0.0 copy-start.9
  261.9 5.2 %fusion.7 = f32[512,1536]{1,0:T(8,128)S(1)} fusion(bf16[2,1536,1536]{1,2,0:T(8,128)(2,1)} %all-gather.8.cloned.1.call-done, bf16[512,1536]{1,0:T(8,128)(2,1)S(1)} %get-tuple-element.85, f32[1536]{0:T(1024)S(1)} %copy-done.10, f32[512]{0:T(512)S(1)} %add_rsqrt_fusion.1, f32[512]{0:T(512)S(1)} %broadcast_multiply_fusion.1), kind=kOutput, calls=%fused_computation.13 | convolution fusion | flops 2421424128 | bytes 9447424 | tf_op jit(solution)/shard_map/dot_general | solution.py:51
  267.1 0.0 copy-done.9
  267.1 0.0 copy-start.2
  267.1 0.0 copy-start.3
  267.1 0.0 copy-start.4
  267.1 0.0 copy-start.5
  267.2 0.0 copy-start.6
  267.2 0.0 copy-start.7
  267.2 2.7 fusion.53
  269.9 0.0 copy-done.2
  269.9 0.0 copy-done.3
  269.9 0.0 copy-done.4
  269.9 0.0 copy-done.5
  269.9 0.0 copy-done.6
  269.9 0.0 copy-done.7
  269.9 24.0 %fusion.83 = (f32[512]{0:T(512)S(1)}, f32[512,1536]{1,0:T(8,128)S(1)}) fusion(f32[1536]{0:T(1024)S(1)} %copy-done.6, pred[512]{0:T(512)(128)(4,1)S(1)} %get-tuple-element.48, f32[1536]{0:T(1024)S(1)} %copy-done.7, pred[512]{0:T(512)(128)(4,1)S(1)} %get-tuple-element.49, f32[1536]{0:T(1024)S(1)} %get-tuple-element.6, ...), kind=kLoop, calls=%fused_computation.211 | loop fusion | flops 73137664 | bytes 6499840 | tf_op jit(solution)/shard_map/reduce_sum | solution.py:30
  293.9 0.0 copy-start.8
  294.0 0.4 multiply_reduce_fusion
  294.4 0.2 copy-done.8
  294.6 2.2 multiply_convert_fusion
  (11 shorter events, 0.1 us)
Async XLA Ops:
  6.5 109.4 %all-gather.4.cloned.1.call-start = ((), (), s32[]{:S(2)}) async-start(), calls=%async_computation | async-start | bytes 1597440 | tf_op jit(solution)/shard_map/all_gather | solution.py:91
  7.3 191.6 %all-gather.6.cloned.1.call-start = ((), (), s32[]{:S(2)}) async-start(), calls=%async_computation.1 | async-start | bytes 1597440 | tf_op jit(solution)/shard_map/all_gather | solution.py:92
  8.0 253.9 %all-gather.8.cloned.1.call-start = ((), (), s32[]{:S(2)}) async-start(), calls=%async_computation.2 | async-start | bytes 10616832 | tf_op jit(solution)/shard_map/all_gather | solution.py:118
  8.7 30.2 %copy-start.1 = (f32[31,1536]{1,0:T(8,128)S(1)}, f32[31,1536]{1,0:T(8,128)}, u32[]{:S(2)}) copy-start(f32[31,1536]{1,0:T(8,128)} %param.15) | copy-start | bytes 571396
  22.2 19.0 %collective-permute-start = (bf16[256,1024]{1,0:T(8,128)(2,1)S(1)}, bf16[256,1024]{1,0:T(8,128)(2,1)S(1)}, u32[]{:S(2)}, u32[]{:S(2)}) collective-permute-start(bf16[256,1024]{1,0:T(8,128)(2,1)S(1)} %get-tuple-element.44), channel_id=1, source_target_pairs={{0,128},{8,136},{16,144},{24,152},{32,160},{40,168},{48,176},{56,1... | collective-permute-start | bytes 1572872 | tf_op jit(solution)/shard_map/ppermute | solution.py:10
  27.3 41.5 %collective-permute-start.1 = (bf16[256,1024]{1,0:T(8,128)(2,1)S(1)}, bf16[256,1024]{1,0:T(8,128)(2,1)}, u32[]{:S(2)}, u32[]{:S(2)}) collective-permute-start(bf16[256,1024]{1,0:T(8,128)(2,1)S(1)} %get-tuple-element.45), channel_id=1, source_target_pairs={{0,256},{8,264},{16,272},{24,280},{32,288},{40,296},{48,304},{56,3... | collective-permute-start | bytes 1572872 | tf_op jit(solution)/shard_map/ppermute | solution.py:10
  33.0 47.8 %collective-permute-start.2 = (bf16[256,1024]{1,0:T(8,128)(2,1)S(1)}, bf16[256,1024]{1,0:T(8,128)(2,1)}, u32[]{:S(2)}, u32[]{:S(2)}) collective-permute-start(bf16[256,1024]{1,0:T(8,128)(2,1)S(1)} %get-tuple-element.46), channel_id=1, source_target_pairs={{0,384},{8,392},{16,400},{24,408},{32,416},{40,424},{48,432},{56,4... | collective-permute-start | bytes 1572872 | tf_op jit(solution)/shard_map/ppermute | solution.py:10
  41.2 39.5 %copy-start = (bf16[256,1024]{1,0:T(8,128)(2,1)}, bf16[256,1024]{1,0:T(8,128)(2,1)S(1)}, u32[]{:S(2)}) copy-start(bf16[256,1024]{1,0:T(8,128)(2,1)S(1)} %collective-permute-done) | copy-start | bytes 1572868
  120.0 142.0 %copy-start.10 = (f32[1536]{0:T(1024)S(1)}, f32[1536]{0:T(1024)}, u32[]{:S(2)}) copy-start(f32[1536]{0:T(1024)} %param.16) | copy-start | bytes 18436
  261.9 5.2 %copy-start.9 = (bf16[2,1536,1536]{1,2,0:T(8,128)(2,1)S(1)}, bf16[2,1536,1536]{1,2,0:T(8,128)(2,1)}, u32[]{:S(2)}) copy-start(bf16[2,1536,1536]{1,2,0:T(8,128)(2,1)} %all-gather.8.cloned.1.call-done) | copy-start | bytes 28311556
  267.1 2.7 copy-start.2
  267.1 2.7 copy-start.3
  267.1 2.7 copy-start.4
  267.1 2.7 copy-start.5
  267.2 2.7 copy-start.6
  267.2 2.7 copy-start.7
  293.9 0.7 copy-start.8
Sparse Core Ops, SparseCore 0:
  10.4 105.5 all-gather.3
  119.0 79.7 all-gather.5
  201.0 60.9 all-gather.7
where the time goes:
time: 304 us; the launch traced here: 303 us
  waiting for transfers between devices  212 us (70%)
  other arithmetic  31.5 us (10%)
  between operations  21 us (7%)
  starting transfers between devices  15.8 us (5%)
  matrix products  15 us (5%)
  local copies, waits for them, and re-layouts  7.95 us (3%)
    all_gather x1, waiting for transfers between devices, body(): lax.all_gather(proj_weight, 'dp', axis=0, tiled=True)  78.9 us
    all_gather x1, waiting for transfers between devices, body(): weight_part = lax.all_gather(point_weight, 'fsdp', axis=2, tiled=True)  59.3 us
    ppermute x3, waiting for transfers between devices, passed_along(): return lax.ppermute(value, axis, pairs)  40.6 us
    all_gather x1, waiting for transfers between devices, body(): lax.all_gather(conv_weight, 'dp', axis=0, tiled=True)  31.2 us
    reduce_sum x1, other arithmetic, layer_norm(): centered = values - jnp.mean(values, axis=-1, keepdims=True)  24 us
    ppermute x3, starting transfers between devices, passed_along(): return lax.ppermute(value, axis, pairs)  15.7 us
  transfers between devices with their start and end apart: 6, of which 6 were waited for; matrix products, arithmetic and copies ran while one was open for 7% of the time, Pallas kernels for 0%

commit v1 on v0

v1 whole, which is shorter than its diff:
```python
import functools

import jax
import jax.numpy as jnp
from jax import lax
from jax.experimental import pallas as pl
from jax.experimental.pallas import tpu as pltpu
from jax.sharding import PartitionSpec as P

GAP = 16
BF16 = jnp.bfloat16
F32 = jnp.float32


def shifted(value, axis, steps):
    count = lax.axis_size(axis)
    pairs = [(source, (source + steps) % count) for source in range(count)]
    return lax.ppermute(value, axis, pairs)


def core_swapped(value, axis):
    count = lax.axis_size(axis)
    return lax.ppermute(value, axis, [(j, j ^ 1) for j in range(count)])


def spread(value, axis, groups):
    size = len(groups[0])
    copies = jnp.broadcast_to(value[None], (size,) + value.shape)
    return lax.all_to_all(copies, axis, 0, 0, axis_index_groups=groups)


def as_bf16(mask):
    return jnp.where(mask, 1.0, 0.0).astype(BF16)


def iota(shape, axis):
    return lax.broadcasted_iota(jnp.int32, shape, axis)


def arriving(own, pair_ref, dest_ref, node_count):
    utts = pair_ref.shape[0]
    spacing = node_count // utts
    sources, lengths = [], []
    for slot in range(utts):
        source = lax.rem(own + node_count - slot * spacing, node_count)
        length = jnp.int32(0)
        for utt in range(utts):
            length += jnp.where(dest_ref[utt, source] == own, pair_ref[utt, source], 0)
        sources.append(source)
        lengths.append(length)
    starts, padded_starts = [], []
    for slot in range(utts):
        start, padded_start = jnp.int32(0), jnp.int32(0)
        for other in range(utts):
            if other != slot:
                before = sources[other] < sources[slot]
                start += jnp.where(before, lengths[other], 0)
                padded_start += jnp.where(before, lengths[other] + GAP, 0)
        starts.append(start)
        padded_starts.append(padded_start)
    return lengths, starts, padded_starts


def cut_kernel(node_count, place_ref, pair_ref, dest_ref, frames_ref, *out_refs):
    own = place_ref[0]
    utts = len(out_refs)
    spacing = node_count // utts
    slot_rows = out_refs[0].shape[0]
    frame_count, channels = frames_ref.shape
    offset = jnp.int32(0)
    starts = [jnp.int32(0)] * utts
    for utt in range(utts):
        for slot in range(utts):
            target = lax.rem(own + slot * spacing, node_count)
            starts[slot] += jnp.where(dest_ref[utt, own] == target, offset, 0)
        offset += pair_ref[utt, own]
    shape = (slot_rows, frame_count)
    ahead = iota(shape, 1) - 2 * iota(shape, 0)
    for slot in range(utts):
        for parity in range(2):
            chosen = as_bf16(ahead == 2 * starts[slot] + parity)
            rows = jnp.dot(chosen, frames_ref[...], preferred_element_type=F32)
            out_refs[slot][:, parity * channels : (parity + 1) * channels] = rows.astype(BF16)


def pack_kernel(node_count, place_ref, pair_ref, dest_ref, *refs):
    piece_refs, out_ref = refs[:-1], refs[-1]
    rows = out_ref.shape[0]
    slot_rows, width = piece_refs[0].shape
    channels = width // 2
    lengths, _, padded_starts = arriving(place_ref[0], pair_ref, dest_ref, node_count)
    shape = (rows, slot_rows)
    behind = iota(shape, 0) - iota(shape, 1)
    within = iota(shape, 1)
    both = jnp.zeros((rows, width), F32)
    earlier = jnp.zeros((rows, channels), F32)
    for slot, piece_ref in enumerate(piece_refs):
        here = as_bf16((behind == padded_starts[slot]) & (within < lengths[slot]))
        both += jnp.dot(here, piece_ref[...], preferred_element_type=F32)
        later = as_bf16((behind == padded_starts[slot] + 1) & (within < lengths[slot] - 1))
        earlier += jnp.dot(later, piece_ref[:, channels:], preferred_element_type=F32)
    out_ref[:, :channels] = earlier.astype(BF16)
    out_ref[:, channels:] = both.astype(BF16)


def layer_norm(values, scales):
    centered = values - jnp.mean(values, axis=-1, keepdims=True)
    variance = jnp.mean(centered * centered, axis=-1, keepdims=True)
    return centered * lax.rsqrt(variance + 1e-05) * scales


def front_kernel(place_ref, xs_ref, parts_ref, gain_ref, out_ref, conv_ref, proj_ref):
    count, part_rows, lanes = parts_ref.shape
    half = count // 2
    chips = count // 2
    position = place_ref[1]
    chip, core = position // 2, lax.rem(position, 2)

    def part(index):
        away = lax.rem(index // 2 + chips - chip, chips)
        other_core = jnp.where(core == index % 2, 0, chips)
        return parts_ref[away + other_core]

    tiles = proj_ref.shape[1] // (half * lanes)
    for index in range(half):
        conv_ref[:, index * lanes : (index + 1) * lanes] = part(index)
    blocks = part_rows // (8 * tiles)
    for index in range(half):
        split = part(half + index).astype(F32).reshape(blocks, tiles, 8, lanes)
        for tile in range(tiles):
            at = (index * tiles + tile) * lanes
            piece = split[:, tile].reshape(blocks * 8, lanes)
            proj_ref[:, at : at + lanes] = piece.astype(BF16)
    front = jnp.dot(xs_ref[...], conv_ref[...], preferred_element_type=F32)
    front = jnp.maximum(front, 0.0).astype(BF16)
    projected = jnp.dot(front, proj_ref[...], preferred_element_type=F32)
    projected = projected.astype(BF16).astype(F32)
    out_ref[...] = layer_norm(projected, gain_ref[...]).astype(BF16)


def mix_kernel(
    node_count,
    place_ref,
    pair_ref,
    dest_ref,
    normed_ref,
    weight_ref,
    depth_ref,
    gain_ref,
    out_ref,
    gated_ref,
    mixed_ref,
):
    step = pl.program_id(0)
    rows = normed_ref.shape[0]
    block = weight_ref.shape[1]
    taps = depth_ref.shape[0]
    contract = (((1,), (1,)), ((), ()))
    value = lax.dot_general(
        normed_ref[...], weight_ref[0], contract, preferred_element_type=F32
    )
    gate = lax.dot_general(
        normed_ref[...], weight_ref[1], contract, preferred_element_type=F32
    )
    gated_ref[pl.ds(0, GAP), :] = jnp.zeros((GAP, block), F32)
    gated_ref[pl.ds(GAP + rows, GAP), :] = jnp.zeros((GAP, block), F32)
    gated = (value * jax.nn.sigmoid(gate)).astype(BF16)
    gated_ref[pl.ds(GAP, rows), :] = gated.astype(F32)
    span = 56
    for lane in range(0, block, 128):
        lanes = slice(lane, lane + 128)
        for row in range(0, rows, span):
            near = gated_ref[row : row + span + 32, lanes]
            total = None
            for low in range(7, -1, -1):
                partial = None
                for high in range(0, 32, 8):
                    tap = high + low - 1
                    if 0 <= tap < taps:
                        term = near[high : high + span + 8] * depth_ref[tap : tap + 1, lanes]
                        partial = term if partial is None else partial + term
                if total is None:
                    total = partial
                else:
                    total = partial + pltpu.roll(total, span + 7, 0)
            at = pl.multiple_of(step * block + lane, 128)
            mixed_ref[row : row + span, pl.ds(at, 128)] = total[:span]

    @pl.when(step == pl.num_programs(0) - 1)
    def _():
        scaled = layer_norm(mixed_ref[...], gain_ref[...])
        encoded = (scaled * jax.nn.sigmoid(scaled)).astype(BF16)
        _, starts, _ = arriving(place_ref[0], pair_ref, dest_ref, node_count)
        out_rows = out_ref.shape[0]
        shape = (out_rows, rows)
        row_ids = iota(shape, 0)
        target = row_ids - GAP
        for start in starts:
            target += jnp.where(row_ids >= start, GAP, 0)
        chosen = as_bf16(iota(shape, 1) == target)
        out_ref[...] = jnp.dot(chosen, encoded, preferred_element_type=F32).astype(BF16)


SMEM = pl.BlockSpec(memory_space=pltpu.SMEM)
VMEM = pl.BlockSpec(memory_space=pltpu.VMEM)


def params():
    return pltpu.CompilerParams(vmem_limit_bytes=40 * 2**20)


def body(
    frames,
    utt_pairs,
    utt_dest,
    conv_weight,
    proj_weight,
    point_weight,
    depth_weight,
    gain_first,
    gain_second,
):
    node_count = lax.axis_size("dp")
    position = lax.axis_index("fsdp")
    frame_count, channels = frames.shape
    pair_count = frame_count // 2
    utts = utt_pairs.shape[2]
    spacing = node_count // utts
    slot_rows = pair_count // 2
    width = proj_weight.shape[1]
    place = jnp.stack([lax.axis_index("dp"), position]).astype(jnp.int32)
    pair_table = utt_pairs[0].T
    dest_table = utt_dest[0].T
    rows = pair_count + (utts - 1) * GAP

    weight_rows = jnp.swapaxes(point_weight, 1, 2)
    weight_full = lax.all_gather(weight_rows, "fsdp", axis=1, tiled=True)

    pieces = pl.pallas_call(
        functools.partial(cut_kernel, node_count),
        out_shape=[jax.ShapeDtypeStruct((slot_rows, 2 * channels), BF16)] * utts,
        in_specs=[SMEM, SMEM, SMEM, VMEM],
        out_specs=[VMEM] * utts,
        compiler_params=params(),
        name="cut",
    )(place, pair_table, dest_table, frames)
    arrived = [pieces[0]]
    for slot in range(1, utts):
        arrived.append(shifted(pieces[slot], "dp", slot * spacing))

    half = 4
    lanes = channels // half
    conv_split = conv_weight.reshape(conv_weight.shape[0], half, lanes)
    conv_part = lax.dynamic_slice_in_dim(conv_weight, (position % half) * lanes, lanes, 1)
    proj_rows = proj_weight.shape[0]
    tiles = width // (half * lanes)
    proj_part = lax.dynamic_slice_in_dim(
        proj_weight, (position % half) * tiles * lanes, tiles * lanes, 1
    )
    proj_part = jnp.concatenate(
        [proj_part[:, t * lanes : (t + 1) * lanes] for t in range(tiles)], axis=0
    )
    own_part = jnp.where(position < half, conv_part, proj_part)
    side = 8
    y_groups = [[y * side + z for y in range(side)] for z in range(side)]
    z_groups = [[y * side + z for z in range(side)] for y in range(side)]
    piece_rows = own_part.shape[0]
    by_y = spread(own_part, "dp", y_groups).reshape(side * piece_rows, lanes)
    by_z = spread(by_y, "dp", z_groups)
    by_z = by_z.reshape(side, side, piece_rows, lanes).swapaxes(0, 1)
    mine = by_z.reshape(side * side * piece_rows, lanes)
    following = shifted(mine, "fsdp", -2)
    opposite = shifted(mine, "fsdp", 4)
    preceding = shifted(mine, "fsdp", 2)
    same = jnp.stack([mine, following, opposite, preceding])
    parts = jnp.concatenate([same, core_swapped(same, "fsdp")])

    packed = pl.pallas_call(
        functools.partial(pack_kernel, node_count),
        out_shape=jax.ShapeDtypeStruct((rows, 3 * channels), BF16),
        in_specs=[SMEM, SMEM, SMEM] + [VMEM] * utts,
        out_specs=VMEM,
        compiler_params=params(),
        name="pack",
    )(place, pair_table, dest_table, *arrived)
    normed = pl.pallas_call(
        front_kernel,
        out_shape=jax.ShapeDtypeStruct((rows, width), BF16),
        in_specs=[SMEM, VMEM, VMEM, VMEM],
        out_specs=VMEM,
        scratch_shapes=[
            pltpu.VMEM((3 * channels, channels), BF16),
            pltpu.VMEM((channels, width), BF16),
        ],
        compiler_params=params(),
        name="front",
    )(place, packed, parts, gain_first[None])

    block = 256
    taps = depth_weight.shape[0]
    return pl.pallas_call(
        functools.partial(mix_kernel, node_count),
        out_shape=jax.ShapeDtypeStruct((pair_count, width), BF16),
        grid=(width // block,),
        in_specs=[
            SMEM,
            SMEM,
            SMEM,
            pl.BlockSpec((rows, width), lambda n: (0, 0)),
            pl.BlockSpec((2, block, width), lambda n: (0, n, 0)),
            pl.BlockSpec((taps, block), lambda n: (0, n)),
            pl.BlockSpec((1, width), lambda n: (0, 0)),
        ],
        out_specs=pl.BlockSpec((pair_count, width), lambda n: (0, 0)),
        scratch_shapes=[
            pltpu.VMEM((rows + 2 * GAP, block), F32),
            pltpu.VMEM((rows, width), F32),
        ],
        compiler_params=params(),
        name="mix",
    )(place, pair_table, dest_table, normed, weight_full, depth_weight, gain_second[None])


def solution(mesh):
    in_specs = (
        P(("dp", "fsdp"), None),
        P("fsdp", None, None),
        P("fsdp", None, None),
        P("dp", None),
        P("dp", None),
        P(None, None, "fsdp"),
        P(),
        P(),
        P(),
    )
    out_specs = P(("dp", "fsdp"), None)
    return jax.shard_map(body, mesh=mesh, in_specs=in_specs, out_specs=out_specs, check_vma=False)
```

time: 304 us -> 139 us (0.46)
  waiting for transfers between devices: 212 us -> 38.1 us
  Pallas kernels: 0 us -> 31 us
  other arithmetic: 31.5 us -> 0.97 us
  starting transfers between devices: 15.8 us -> 32.3 us
  matrix products: 15 us -> 0 us
  blocking collectives: 0 us -> 14.5 us
  between operations: 21 us -> 13.7 us
    all_gather x3 -> x1, waiting for transfers between devices: 169 us -> 0.02 us  [body(): weight_full = lax.all_gather(weight_rows, 'fsdp', axis=1, tiled=True)]
    pallas_call x0 -> x4, Pallas kernels: none -> 31 us  [the longest x1 21.3 us: body(): pl.pallas_call(functools.partial(mix_kernel, node_count), out_shape=jax.S...]
    reduce_sum x6 -> x0, other arithmetic: 26 us -> none  [the longest x1 24 us: layer_norm(): centered = values - jnp.mean(values, axis=-1, keepdims=True)]
    dot_general x5 -> x0, matrix products: 15 us -> none  [the longest x1 5.16 us: gate_product(): gate_part = jnp.dot(normed, gate_weight, preferred_element_type=jnp.float32)]
    all_to_all x0 -> x1, blocking collectives: none -> 14.5 us  [spread(): return lax.all_to_all(copies, axis, 0, 0, axis_index_groups=groups)]
    all_to_all x0 -> x1, starting transfers between devices: none -> 10 us  [spread(): return lax.all_to_all(copies, axis, 0, 0, axis_index_groups=groups)]
    ppermute x3 -> x7, starting transfers between devices: 15.7 us -> 22.2 us  [the longest x6 19.7 us: shifted(): return lax.ppermute(value, axis, pairs)]
    unnamed x22, local copies, waits for them, and re-layouts: 0.26 us -> 5.25 us
  transfers between devices with their start and end apart: 6 -> 9, of which waited for: 6 -> 4; matrix products, arithmetic and copies ran while one was open for 7% -> 3% of each run, Pallas kernels for 0% -> 7%
where the time goes in v1:
time: 139 us
  waiting for transfers between devices  38.1 us (27%)
  starting transfers between devices  32.3 us (23%)
  Pallas kernels  31 us (22%)
  blocking collectives  14.5 us (10%)
  between operations  13.7 us (10%)
  local copies, waits for them, and re-layouts  8.04 us (6%)
    ppermute x6, waiting for transfers between devices, shifted(): return lax.ppermute(value, axis, pairs)  34.8 us
    pallas_call x1, Pallas kernels, body(): pl.pallas_call(functools.partial(mix_kernel, node_count), out_shape=jax.S...  21.3 us
    ppermute x6, starting transfers between devices, shifted(): return lax.ppermute(value, axis, pairs)  19.7 us
    all_to_all x1, blocking collectives, spread(): return lax.all_to_all(copies, axis, 0, 0, axis_index_groups=groups)  14.5 us
    all_to_all x1, starting transfers between devices, spread(): return lax.all_to_all(copies, axis, 0, 0, axis_index_groups=groups)  10 us
    unnamed x22, local copies, waits for them, and re-layouts  5.25 us
    pallas_call x1, Pallas kernels, body(): pl.pallas_call(front_kernel, out_shape=jax.ShapeDtypeStruct((rows, width)...  3.63 us
    pallas_call x1, Pallas kernels, body(): pl.pallas_call(functools.partial(cut_kernel, node_count), out_shape=[jax....  3.51 us
  transfers between devices with their start and end apart: 9, of which 4 were waited for; matrix products, arithmetic and copies ran while one was open for 3% of the time, Pallas kernels for 7%

profile of v1, /device:TPU:1, one launch (start us, length us, event | category | flops | bytes accessed | tf_op | source)
XLA Modules:
  0.0 138.5 jit_solution(1731651159929854045)
XLA Ops:
  6.5 0.0 copy-start.4
  6.5 0.0 copy-start.6
  6.5 0.0 copy-start.1
  6.5 0.0 copy-start.7
  6.5 0.0 copy-start.8
  6.5 0.0 all-gather.2.cloned.1.call-start
  6.6 0.7 all-gather.2.cloned.1.call-update
  7.3 0.7 constant_dynamic-slice_fusion.1
  8.0 0.7 maximum_select_fusion
  8.7 14.5 %all_to_all.10 = bf16[8,24,128]{2,1,0:T(8,128)(2,1)S(1)} all-to-all(bf16[8,24,128]{2,1,0:T(8,128)(2,1)S(1)} %broadcast_in_dim.19), channel_id=1, replica_groups={{0,64,128,192,256,320,384,448},{8,72,136,200,264,328,392,456},{16,80,14..., dimensions={0} | all-to-all | bytes 98304 | tf_op jit(solution)/shard_map/all_to_all | solution.py:29
  23.2 0.8 broadcast_in_dim.21
  24.0 10.0 %all-to-all-start.1 = ((bf16[8,192,128]{2,1,0:T(8,128)(2,1)}), bf16[8,192,128]{2,1,0:T(8,128)(2,1)}, u32[]{:S(2)}, u32[]{:S(2)}) async-start(bf16[8,192,128]{2,1,0:T(8,128)(2,1)} %broadcast_in_dim.21), calls=%async_computation.1 | async-start | bytes 786432 | tf_op jit(solution)/shard_map/all_to_all | solution.py:29
  34.1 0.1 pad_add_fusion.place_ref
  34.1 0.0 copy-done.1
  34.2 0.0 copy-start.3
  34.2 0.7 copy-done.3
  34.8 0.0 copy-start.5
  34.8 0.7 copy-done.5
  35.5 3.5 %cut.1 = (bf16[256,1024]{1,0:T(8,128)(2,1)S(1)}, bf16[256,1024]{1,0:T(8,128)(2,1)}, bf16[256,1024]{1,0:T(8,128)(2,1)S(1)}, bf16[256,1024]{1,0:T(8,128)(2,1)S(1)}) custom-call(s32[2]{0:T(128)S(1)} %pad_add_fusion.place_ref, s32[4,64]{1,0:T(4,128)S(1)} %bitcast.21, s32[4,64]{1,0:T(4,128)S(1)} %bitcast.24, bf16[1024,512]{1,0:T(8,128)(2,1)S(1)} %copy-done.1), custom_call_target="tpu_custom_call" | custom-call | tf_op jit(solution)/shard_map/cut/pallas_call | solution.py:239
  39.0 2.1 %collective-permute-start = (bf16[256,1024]{1,0:T(8,128)(2,1)}, bf16[256,1024]{1,0:T(8,128)(2,1)S(1)}, u32[]{:S(2)}, u32[]{:S(2)}) collective-permute-start(bf16[256,1024]{1,0:T(8,128)(2,1)} %get-tuple-element.10), channel_id=1, source_target_pairs={{0,128},{8,136},{16,144},{24,152},{32,160},{40,168},{48,176},{56,1... | collective-permute-start | bytes 1572872 | tf_op jit(solution)/shard_map/ppermute | solution.py:18
  41.2 4.0 %collective-permute-start.1 = (bf16[256,1024]{1,0:T(8,128)(2,1)S(1)}, bf16[256,1024]{1,0:T(8,128)(2,1)S(1)}, u32[]{:S(2)}, u32[]{:S(2)}) collective-permute-start(bf16[256,1024]{1,0:T(8,128)(2,1)S(1)} %get-tuple-element.11), channel_id=1, source_target_pairs={{0,256},{8,264},{16,272},{24,280},{32,288},{40,296},{48,304},{56,3... | collective-permute-start | bytes 1572872 | tf_op jit(solution)/shard_map/ppermute | solution.py:18
  45.1 3.7 %collective-permute-start.2 = (bf16[256,1024]{1,0:T(8,128)(2,1)S(1)}, bf16[256,1024]{1,0:T(8,128)(2,1)S(1)}, u32[]{:S(2)}, u32[]{:S(2)}) collective-permute-start(bf16[256,1024]{1,0:T(8,128)(2,1)S(1)} %get-tuple-element.12), channel_id=1, source_target_pairs={{0,384},{8,392},{16,400},{24,408},{32,416},{40,424},{48,432},{56,4... | collective-permute-start | bytes 1572872 | tf_op jit(solution)/shard_map/ppermute | solution.py:18
  48.9 0.0 all-to-all-done.1
  48.9 1.0 copy.10
  49.9 4.4 %collective-permute-start.3 = (bf16[1536,128]{1,0:T(8,128)(2,1)S(1)}, bf16[1536,128]{1,0:T(8,128)(2,1)S(1)}, u32[]{:S(2)}, u32[]{:S(2)}) collective-permute-start(bf16[1536,128]{1,0:T(8,128)(2,1)S(1)} %bitcast.27), channel_id=1, source_target_pairs={{0,6},{1,7},{2,0},{3,1},{4,2},{5,3},{6,4},{7,5},{8,14},{9,15},{10,... | collective-permute-start | bytes 1179656 | tf_op jit(solution)/shard_map/ppermute | solution.py:18
  54.3 2.4 %collective-permute-start.4 = (bf16[1536,128]{1,0:T(8,128)(2,1)S(1)}, bf16[1536,128]{1,0:T(8,128)(2,1)S(1)}, u32[]{:S(2)}, u32[]{:S(2)}) collective-permute-start(bf16[1536,128]{1,0:T(8,128)(2,1)S(1)} %bitcast.28), channel_id=1, source_target_pairs={{0,4},{1,5},{2,6},{3,7},{4,0},{5,1},{6,2},{7,3},{8,12},{9,13},{10,... | collective-permute-start | bytes 1179656 | tf_op jit(solution)/shard_map/ppermute | solution.py:18
  56.7 7.7 %collective-permute-done.refs_1_ = bf16[256,1024]{1,0:T(8,128)(2,1)S(1)} collective-permute-done((bf16[256,1024]{1,0:T(8,128)(2,1)}, bf16[256,1024]{1,0:T(8,128)(2,1)S(1)}, u32[]{:S(2)}, u32[]{:S(2)}) %collective-permute-start) | collective-permute-done | bytes 524320 | tf_op jit(solution)/shard_map/ppermute | solution.py:18
  64.4 3.0 %collective-permute-start.5 = (bf16[1536,128]{1,0:T(8,128)(2,1)S(1)}, bf16[1536,128]{1,0:T(8,128)(2,1)S(1)}, u32[]{:S(2)}, u32[]{:S(2)}) collective-permute-start(bf16[1536,128]{1,0:T(8,128)(2,1)S(1)} %bitcast.29), channel_id=1, source_target_pairs={{0,2},{1,3},{2,4},{3,5},{4,6},{5,7},{6,0},{7,1},{8,10},{9,11},{10,... | collective-permute-start | bytes 1179656 | tf_op jit(solution)/shard_map/ppermute | solution.py:18
  67.5 0.0 copy-done.7
  67.5 0.0 copy-done.8
  67.5 12.0 %collective-permute-done.1.refs_2_ = bf16[256,1024]{1,0:T(8,128)(2,1)S(1)} collective-permute-done((bf16[256,1024]{1,0:T(8,128)(2,1)S(1)}, bf16[256,1024]{1,0:T(8,128)(2,1)S(1)}, u32[]{:S(2)}, u32[]{:S(2)}) %collective-permute-start.1) | collective-permute-done | bytes 524320 | tf_op jit(solution)/shard_map/ppermute | solution.py:18
  79.5 15.1 %collective-permute-done.2.refs_3_ = bf16[256,1024]{1,0:T(8,128)(2,1)S(1)} collective-permute-done((bf16[256,1024]{1,0:T(8,128)(2,1)S(1)}, bf16[256,1024]{1,0:T(8,128)(2,1)S(1)}, u32[]{:S(2)}, u32[]{:S(2)}) %collective-permute-start.2) | collective-permute-done | bytes 524320 | tf_op jit(solution)/shard_map/ppermute | solution.py:18
  94.6 0.0 copy-done.4
  94.6 0.0 copy-done.6
  94.6 2.6 %pack.1.xs_ref = bf16[560,1536]{1,0:T(8,128)(2,1)S(1)} custom-call(s32[2]{0:T(128)S(1)} %pad_add_fusion.place_ref, s32[4,64]{1,0:T(4,128)S(1)} %bitcast.22, s32[4,64]{1,0:T(4,128)S(1)} %bitcast.25, bf16[256,1024]{1,0:T(8,128)(2,1)S(1)} %get-tuple-element.9.refs_0_, bf16[256,1024]{1,0:T(8,128)(2,1)S(1)} %collective-permute-done.refs_1_, ...), custom_call_target="tpu_custom_call" | custom-call | tf_op jit(solution)/shard_map/pack/pallas_call | solution.py:278
  97.2 0.0 collective-permute-done.3
  97.2 0.0 collective-permute-done.4
  97.2 0.0 collective-permute-done.5
  97.2 0.2 pad_maximum_fusion
  97.4 2.6 %collective-permute-start.6 = (bf16[4,1536,128]{2,1,0:T(8,128)(2,1)S(1)}, bf16[4,1536,128]{2,1,0:T(8,128)(2,1)S(1)}, u32[]{:S(2)}, u32[]{:S(2)}) collective-permute-start(bf16[4,1536,128]{2,1,0:T(8,128)(2,1)S(1)} %pad_maximum_fusion), channel_id=1, source_target_pairs={{0,1},{1,0},{2,3},{3,2},{4,5},{5,4},{6,7},{7,6},{8,9},{9,8},{10,11... | collective-permute-start | bytes 4718600 | tf_op jit(solution)/shard_map/ppermute | solution.py:23
  100.1 0.1 constant_dynamic-update-slice_fusion.3
  100.1 0.1 constant_dynamic-update-slice_fusion.2
  100.2 0.1 constant_dynamic-update-slice_fusion.1
  100.2 2.6 %collective-permute-done.6 = bf16[4,1536,128]{2,1,0:T(8,128)(2,1)S(1)} collective-permute-done((bf16[4,1536,128]{2,1,0:T(8,128)(2,1)S(1)}, bf16[4,1536,128]{2,1,0:T(8,128)(2,1)S(1)}, u32[]{:S(2)}, u32[]{:S(2)}) %collective-permute-start.6) | collective-permute-done | bytes 1572896 | tf_op jit(solution)/shard_map/ppermute | solution.py:23
  102.9 0.2 constant_dynamic-update-slice_fusion.parts_ref
  103.1 0.0 copy-start.2
  103.1 3.6 %front.1.normed_ref = bf16[560,1536]{1,0:T(8,128)(2,1)S(1)} custom-call(s32[2]{0:T(128)S(1)} %pad_add_fusion.place_ref, bf16[560,1536]{1,0:T(8,128)(2,1)S(1)} %pack.1.xs_ref, bf16[8,1536,128]{2,1,0:T(8,128)(2,1)S(1)} %constant_dynamic-update-slice_fusion.parts_ref, f32[1,1536]{1,0:T(1,128)S(1)} %broadcast_in_dim.22.gain_ref), custom_call_target="tpu_custom_call" | custom-call | tf_op jit(solution)/shard_map/front/pallas_call | solution.py:286
  106.7 0.0 all-gather.2.cloned.1.call-done.weight_ref
  106.8 0.0 copy-done.2
  106.8 0.0 copy-start
  106.8 3.7 %copy-done = bf16[2,1536,1536]{2,1,0:T(8,128)(2,1)S(1)} copy-done((bf16[2,1536,1536]{2,1,0:T(8,128)(2,1)S(1)}, bf16[2,1536,1536]{2,1,0:T(8,128)(2,1)}, u32[]{:S(2)}) %copy-start) | copy-done | bytes 9437208
  110.4 21.3 %mix.1 = bf16[512,1536]{1,0:T(8,128)(2,1)} custom-call(s32[2]{0:T(128)S(1)} %pad_add_fusion.place_ref, s32[4,64]{1,0:T(4,128)S(1)} %bitcast.23, s32[4,64]{1,0:T(4,128)S(1)} %bitcast.26, bf16[560,1536]{1,0:T(8,128)(2,1)S(1)} %front.1.normed_ref, bf16[2,1536,1536]{2,1,0:T(8,128)(2,1)S(1)} %copy-done, f32[31,1536]{1,0:T(8,128)S(1)} %copy-done.2, ...), custom_call_target="tpu_custom_call" | custom-call | tf_op jit(solution)/shard_map/mix/pallas_call | solution.py:301
  (4 shorter events, 0.1 us)
Async XLA Ops:
  6.5 88.1 %copy-start.4 = (s32[1,64,4]{1,2,0:T(4,128)S(1)}, s32[1,64,4]{1,2,0:T(4,128)}, u32[]{:S(2)}) copy-start(s32[1,64,4]{1,2,0:T(4,128)} %param.10) | copy-start | bytes 3076
  6.5 88.1 %copy-start.6 = (s32[1,64,4]{1,2,0:T(4,128)S(1)}, s32[1,64,4]{1,2,0:T(4,128)}, u32[]{:S(2)}) copy-start(s32[1,64,4]{1,2,0:T(4,128)} %param.11) | copy-start | bytes 3076
  6.5 27.6 %copy-start.1 = (bf16[1024,512]{1,0:T(8,128)(2,1)S(1)}, bf16[1024,512]{1,0:T(8,128)(2,1)}, u32[]{:S(2)}) copy-start(bf16[1024,512]{1,0:T(8,128)(2,1)} %frames_ref.1) | copy-start | bytes 3145732
  6.5 60.9 %copy-start.7 = (f32[1536]{0:T(1024)S(1)}, f32[1536]{0:T(1024)}, u32[]{:S(2)}) copy-start(f32[1536]{0:T(1024)} %param.16) | copy-start | bytes 18436
  6.5 61.0 %copy-start.8 = (f32[1536]{0:T(1024)S(1)}, f32[1536]{0:T(1024)}, u32[]{:S(2)}) copy-start(f32[1536]{0:T(1024)} %param.17) | copy-start | bytes 18436
  6.5 100.2 %all-gather.2.cloned.1.call-start = ((), (), s32[]{:S(2)}) async-start(), calls=%async_computation.2 | async-start | bytes 10616832 | tf_op jit(solution)/shard_map/all_gather | solution.py:237
  24.0 24.8 %all-to-all-start.1 = ((bf16[8,192,128]{2,1,0:T(8,128)(2,1)}), bf16[8,192,128]{2,1,0:T(8,128)(2,1)}, u32[]{:S(2)}, u32[]{:S(2)}) async-start(bf16[8,192,128]{2,1,0:T(8,128)(2,1)} %broadcast_in_dim.21), calls=%async_computation.1 | async-start | bytes 786432 | tf_op jit(solution)/shard_map/all_to_all | solution.py:29
  34.2 0.7 copy-start.3
  34.8 0.7 copy-start.5
  39.0 25.4 %collective-permute-start = (bf16[256,1024]{1,0:T(8,128)(2,1)}, bf16[256,1024]{1,0:T(8,128)(2,1)S(1)}, u32[]{:S(2)}, u32[]{:S(2)}) collective-permute-start(bf16[256,1024]{1,0:T(8,128)(2,1)} %get-tuple-element.10), channel_id=1, source_target_pairs={{0,128},{8,136},{16,144},{24,152},{32,160},{40,168},{48,176},{56,1... | collective-permute-start | bytes 1572872 | tf_op jit(solution)/shard_map/ppermute | solution.py:18
  41.2 38.4 %collective-permute-start.1 = (bf16[256,1024]{1,0:T(8,128)(2,1)S(1)}, bf16[256,1024]{1,0:T(8,128)(2,1)S(1)}, u32[]{:S(2)}, u32[]{:S(2)}) collective-permute-start(bf16[256,1024]{1,0:T(8,128)(2,1)S(1)} %get-tuple-element.11), channel_id=1, source_target_pairs={{0,256},{8,264},{16,272},{24,280},{32,288},{40,296},{48,304},{56,3... | collective-permute-start | bytes 1572872 | tf_op jit(solution)/shard_map/ppermute | solution.py:18
  45.1 49.5 %collective-permute-start.2 = (bf16[256,1024]{1,0:T(8,128)(2,1)S(1)}, bf16[256,1024]{1,0:T(8,128)(2,1)S(1)}, u32[]{:S(2)}, u32[]{:S(2)}) collective-permute-start(bf16[256,1024]{1,0:T(8,128)(2,1)S(1)} %get-tuple-element.12), channel_id=1, source_target_pairs={{0,384},{8,392},{16,400},{24,408},{32,416},{40,424},{48,432},{56,4... | collective-permute-start | bytes 1572872 | tf_op jit(solution)/shard_map/ppermute | solution.py:18
  49.9 47.3 %collective-permute-start.3 = (bf16[1536,128]{1,0:T(8,128)(2,1)S(1)}, bf16[1536,128]{1,0:T(8,128)(2,1)S(1)}, u32[]{:S(2)}, u32[]{:S(2)}) collective-permute-start(bf16[1536,128]{1,0:T(8,128)(2,1)S(1)} %bitcast.27), channel_id=1, source_target_pairs={{0,6},{1,7},{2,0},{3,1},{4,2},{5,3},{6,4},{7,5},{8,14},{9,15},{10,... | collective-permute-start | bytes 1179656 | tf_op jit(solution)/shard_map/ppermute | solution.py:18
  54.3 42.9 %collective-permute-start.4 = (bf16[1536,128]{1,0:T(8,128)(2,1)S(1)}, bf16[1536,128]{1,0:T(8,128)(2,1)S(1)}, u32[]{:S(2)}, u32[]{:S(2)}) collective-permute-start(bf16[1536,128]{1,0:T(8,128)(2,1)S(1)} %bitcast.28), channel_id=1, source_target_pairs={{0,4},{1,5},{2,6},{3,7},{4,0},{5,1},{6,2},{7,3},{8,12},{9,13},{10,... | collective-permute-start | bytes 1179656 | tf_op jit(solution)/shard_map/ppermute | solution.py:18
  64.4 32.8 %collective-permute-start.5 = (bf16[1536,128]{1,0:T(8,128)(2,1)S(1)}, bf16[1536,128]{1,0:T(8,128)(2,1)S(1)}, u32[]{:S(2)}, u32[]{:S(2)}) collective-permute-start(bf16[1536,128]{1,0:T(8,128)(2,1)S(1)} %bitcast.29), channel_id=1, source_target_pairs={{0,2},{1,3},{2,4},{3,5},{4,6},{5,7},{6,0},{7,1},{8,10},{9,11},{10,... | collective-permute-start | bytes 1179656 | tf_op jit(solution)/shard_map/ppermute | solution.py:18
  97.4 5.4 %collective-permute-start.6 = (bf16[4,1536,128]{2,1,0:T(8,128)(2,1)S(1)}, bf16[4,1536,128]{2,1,0:T(8,128)(2,1)S(1)}, u32[]{:S(2)}, u32[]{:S(2)}) collective-permute-start(bf16[4,1536,128]{2,1,0:T(8,128)(2,1)S(1)} %pad_maximum_fusion), channel_id=1, source_target_pairs={{0,1},{1,0},{2,3},{3,2},{4,5},{5,4},{6,7},{7,6},{8,9},{9,8},{10,11... | collective-permute-start | bytes 4718600 | tf_op jit(solution)/shard_map/ppermute | solution.py:23
  103.1 3.7 %copy-start.2 = (f32[31,1536]{1,0:T(8,128)S(1)}, f32[31,1536]{1,0:T(8,128)}, u32[]{:S(2)}) copy-start(f32[31,1536]{1,0:T(8,128)} %depth_ref.1) | copy-start | bytes 571396
  106.8 3.7 %copy-start = (bf16[2,1536,1536]{2,1,0:T(8,128)(2,1)S(1)}, bf16[2,1536,1536]{2,1,0:T(8,128)(2,1)}, u32[]{:S(2)}) copy-start(bf16[2,1536,1536]{2,1,0:T(8,128)(2,1)} %all-gather.2.cloned.1.call-done.weight_ref) | copy-start | bytes 28311556
Sparse Core Ops, SparseCore 0:
  9.5 80.8 all-gather.1

commit v2 on v1

v2 whole, which is shorter than its diff:
```python
import functools

import jax
import jax.numpy as jnp
from jax import lax
from jax.experimental import pallas as pl
from jax.experimental.pallas import tpu as pltpu
from jax.sharding import PartitionSpec as P

GAP = 16
BF16 = jnp.bfloat16
F32 = jnp.float32


def shifted(value, axis, steps):
    count = lax.axis_size(axis)
    pairs = [(source, (source + steps) % count) for source in range(count)]
    return lax.ppermute(value, axis, pairs)


def core_swapped(value, axis):
    count = lax.axis_size(axis)
    return lax.ppermute(value, axis, [(j, j ^ 1) for j in range(count)])


def along_z(value, side, steps):
    pairs = [
        (y * side + z, y * side + (z + steps) % side) for y in range(side) for z in range(side)
    ]
    return lax.ppermute(value, "dp", pairs)


def as_bf16(mask):
    return jnp.where(mask, 1.0, 0.0).astype(BF16)


def iota(shape, axis):
    return lax.broadcasted_iota(jnp.int32, shape, axis)


def arriving(own, pair_ref, dest_ref, node_count):
    utts = pair_ref.shape[0]
    spacing = node_count // utts
    sources, lengths = [], []
    for slot in range(utts):
        source = lax.rem(own + node_count - slot * spacing, node_count)
        length = jnp.int32(0)
        for utt in range(utts):
            length += jnp.where(dest_ref[utt, source] == own, pair_ref[utt, source], 0)
        sources.append(source)
        lengths.append(length)
    starts, padded_starts = [], []
    for slot in range(utts):
        start, padded_start = jnp.int32(0), jnp.int32(0)
        for other in range(utts):
            if other != slot:
                before = sources[other] < sources[slot]
                start += jnp.where(before, lengths[other], 0)
                padded_start += jnp.where(before, lengths[other] + GAP, 0)
        starts.append(start)
        padded_starts.append(padded_start)
    return lengths, starts, padded_starts


def own_kernel(place_ref, conv_ref, proj_ref, out_ref):
    copies, part_rows, lanes = out_ref.shape
    proj = proj_ref[...].astype(F32)
    tiles = [proj[:, at : at + lanes] for at in range(0, proj.shape[1], lanes)]
    is_conv = lax.rem(place_ref[1], 2) == 0
    chosen = jnp.where(is_conv, conv_ref[...].astype(F32), jnp.concatenate(tiles, axis=0))
    for copy in range(copies):
        out_ref[copy] = chosen.astype(BF16)


def cut_kernel(node_count, place_ref, pair_ref, dest_ref, frames_ref, *out_refs):
    own = place_ref[0]
    utts = len(out_refs)
    spacing = node_count // utts
    slot_rows = out_refs[0].shape[0]
    frame_count, channels = frames_ref.shape
    offset = jnp.int32(0)
    starts = [jnp.int32(0)] * utts
    for utt in range(utts):
        for slot in range(utts):
            target = lax.rem(own + slot * spacing, node_count)
            starts[slot] += jnp.where(dest_ref[utt, own] == target, offset, 0)
        offset += pair_ref[utt, own]
    shape = (slot_rows, frame_count)
    ahead = iota(shape, 1) - 2 * iota(shape, 0)
    for slot in range(utts):
        for parity in range(2):
            chosen = as_bf16(ahead == 2 * starts[slot] + parity)
            rows = jnp.dot(chosen, frames_ref[...], preferred_element_type=F32)
            out_refs[slot][:, parity * channels : (parity + 1) * channels] = rows.astype(BF16)


def pack_kernel(node_count, place_ref, pair_ref, dest_ref, *refs):
    piece_refs, out_ref = refs[:-1], refs[-1]
    rows = out_ref.shape[0]
    slot_rows, width = piece_refs[0].shape
    channels = width // 2
    lengths, _, padded_starts = arriving(place_ref[0], pair_ref, dest_ref, node_count)
    shape = (rows, slot_rows)
    behind = iota(shape, 0) - iota(shape, 1)
    within = iota(shape, 1)
    both = jnp.zeros((rows, width), F32)
    earlier = jnp.zeros((rows, channels), F32)
    for slot, piece_ref in enumerate(piece_refs):
        here = as_bf16((behind == padded_starts[slot]) & (within < lengths[slot]))
        both += jnp.dot(here, piece_ref[...], preferred_element_type=F32)
        later = as_bf16((behind == padded_starts[slot] + 1) & (within < lengths[slot] - 1))
        earlier += jnp.dot(later, piece_ref[:, channels:], preferred_element_type=F32)
    out_ref[:, :channels] = earlier.astype(BF16)
    out_ref[:, channels:] = both.astype(BF16)


def layer_norm(values, scales):
    centered = values - jnp.mean(values, axis=-1, keepdims=True)
    variance = jnp.mean(centered * centered, axis=-1, keepdims=True)
    return centered * lax.rsqrt(variance + 1e-05) * scales


def arrange(offsets, place_ref, mine_ref, other_ref, conv_ref, proj_ref):
    _, columns, part_rows, lanes = mine_ref.shape
    side = len(offsets)
    tiles = part_rows // 8
    core = lax.rem(place_ref[1], 2)
    own = lax.rem(place_ref[0], side)

    def fill(conv_part_ref, proj_part_ref):
        for index, offset in enumerate(offsets):
            row = lax.rem(own + offset + side, side)
            for column in range(columns):
                at = column * side + row
                block = conv_part_ref[index, column].astype(F32)
                conv_ref[pl.ds(pl.multiple_of(at * part_rows, 8), part_rows), :] = block
                block = proj_part_ref[index, column].astype(F32)
                for tile in range(tiles):
                    into = pl.ds(pl.multiple_of(at * 8, 8), 8)
                    piece = block[tile * 8 : (tile + 1) * 8]
                    proj_ref[into, tile * lanes : (tile + 1) * lanes] = piece

    @pl.when(core == 0)
    def _():
        fill(mine_ref, other_ref)

    @pl.when(core == 1)
    def _():
        fill(other_ref, mine_ref)


def depthwise(gated_ref, depth_ref, mixed_ref, lane, at):
    rows = mixed_ref.shape[0]
    taps = depth_ref.shape[0]
    span = 56
    lanes = slice(lane, lane + 128)
    for row in range(0, rows, span):
        near = gated_ref[row : row + span + 32, lanes]
        total = None
        for low in range(7, -1, -1):
            partial = None
            for high in range(0, 32, 8):
                tap = high + low - 1
                if 0 <= tap < taps:
                    weight = depth_ref[tap : tap + 1, at : at + 128]
                    term = near[high : high + span + 8] * weight
                    partial = term if partial is None else partial + term
            if total is None:
                total = partial
            else:
                total = partial + pltpu.roll(total, span + 7, 0)
        mixed_ref[row : row + span, at : at + 128] = total[:span]


def mix_kernel(
    node_count,
    offsets,
    place_ref,
    pair_ref,
    dest_ref,
    xs_ref,
    mine_ref,
    other_ref,
    first_ref,
    depth_ref,
    gain_ref,
    weight_ref,
    out_ref,
    conv_ref,
    proj_ref,
    normed_ref,
    held_ref,
    gated_ref,
    mixed_ref,
    sems,
):
    rows, width = normed_ref.shape
    steps, _, block, _ = held_ref.shape
    copies = []
    for step in range(steps):
        part = weight_ref.at[:, pl.ds(step * block, block), :]
        copies.append(pltpu.make_async_copy(part, held_ref.at[step], sems.at[step]))
    for copy in copies:
        copy.start()

    arrange(offsets, place_ref, mine_ref, other_ref, conv_ref, proj_ref)
    front = jnp.dot(xs_ref[...], conv_ref[...].astype(BF16), preferred_element_type=F32)
    front = jnp.maximum(front, 0.0).astype(BF16)
    projected = jnp.dot(front, proj_ref[...].astype(BF16), preferred_element_type=F32)
    projected = projected.astype(BF16).astype(F32)
    normed_ref[...] = layer_norm(projected, first_ref[...]).astype(BF16)

    for buffer in range(2):
        gated_ref[buffer, pl.ds(0, GAP), :] = jnp.zeros((GAP, block), F32)
        gated_ref[buffer, pl.ds(GAP + rows, GAP), :] = jnp.zeros((GAP, block), F32)
    contract = (((1,), (1,)), ((), ()))

    def multiply(step):
        copies[step].wait()
        value, gate = (
            lax.dot_general(
                normed_ref[...], held_ref[step, part], contract, preferred_element_type=F32
            )
            for part in range(2)
        )
        gated = (value * jax.nn.sigmoid(gate)).astype(BF16)
        gated_ref[step % 2, pl.ds(GAP, rows), :] = gated.astype(F32)

    multiply(0)
    for step in range(steps):
        if step + 1 < steps:
            multiply(step + 1)
        for lane in range(0, block, 128):
            depthwise(gated_ref.at[step % 2], depth_ref, mixed_ref, lane, step * block + lane)

    scaled = layer_norm(mixed_ref[...], gain_ref[...])
    encoded = (scaled * jax.nn.sigmoid(scaled)).astype(BF16)
    _, starts, _ = arriving(place_ref[0], pair_ref, dest_ref, node_count)
    shape = (out_ref.shape[0], rows)
    row_ids = iota(shape, 0)
    target = row_ids - GAP
    for start in starts:
        target += jnp.where(row_ids >= start, GAP, 0)
    chosen = as_bf16(iota(shape, 1) == target)
    out_ref[...] = jnp.dot(chosen, encoded, preferred_element_type=F32).astype(BF16)


SMEM = pl.BlockSpec(memory_space=pltpu.SMEM)
VMEM = pl.BlockSpec(memory_space=pltpu.VMEM)
ANY = pl.BlockSpec(memory_space=pl.ANY)


def params(mebibytes):
    return pltpu.CompilerParams(vmem_limit_bytes=mebibytes * 2**20)


def cost(flops, moved):
    return pl.CostEstimate(flops=flops, bytes_accessed=moved, transcendentals=0)


def body(
    frames,
    utt_pairs,
    utt_dest,
    conv_weight,
    proj_weight,
    point_weight,
    depth_weight,
    gain_first,
    gain_second,
):
    node_count = lax.axis_size("dp")
    position = lax.axis_index("fsdp")
    frame_count, channels = frames.shape
    pair_count = frame_count // 2
    utts = utt_pairs.shape[2]
    spacing = node_count // utts
    slot_rows = pair_count // 2
    width = proj_weight.shape[1]
    place = jnp.stack([lax.axis_index("dp"), position]).astype(jnp.int32)
    pair_table = utt_pairs[0].T
    dest_table = utt_dest[0].T
    rows = pair_count + (utts - 1) * GAP

    weight_rows = jnp.swapaxes(point_weight, 1, 2)
    weight_full = lax.all_gather(weight_rows, "fsdp", axis=1, tiled=True)

    pieces = pl.pallas_call(
        functools.partial(cut_kernel, node_count),
        out_shape=[jax.ShapeDtypeStruct((slot_rows, 2 * channels), BF16)] * utts,
        in_specs=[SMEM, SMEM, SMEM, VMEM],
        out_specs=[VMEM] * utts,
        compiler_params=params(10),
        cost_estimate=cost(4 * 10**9, 4 * 10**6),
        name="cut",
    )(place, pair_table, dest_table, frames)
    arrived = [pieces[0]]
    for slot in range(1, utts):
        arrived.append(shifted(pieces[slot], "dp", slot * spacing))

    side = 8
    y_groups = [[y * side + z for y in range(side)] for z in range(side)]
    copies = pl.pallas_call(
        own_kernel,
        out_shape=jax.ShapeDtypeStruct((side,) + conv_weight.shape, BF16),
        in_specs=[SMEM, VMEM, VMEM],
        out_specs=VMEM,
        compiler_params=params(4),
        cost_estimate=cost(10**5, 3 * 10**5),
        name="own",
    )(place, conv_weight, proj_weight)
    by_y = lax.all_to_all(copies, "dp", 0, 0, axis_index_groups=y_groups)
    by_y, _ = lax.optimization_barrier((by_y, pieces[1]))
    below = along_z(by_y, side, 3)
    above = along_z(by_y, side, -3)
    from_below = along_z(jnp.stack([by_y, above]), side, 1)
    from_above = along_z(jnp.stack([by_y, below, above]), side, -1)
    mine = jnp.concatenate([jnp.stack([by_y, below, above]), from_below, from_above])
    offsets = (0, -3, 3, -1, 2, 1, -2, 4)
    other = core_swapped(mine, "fsdp")
    packed = pl.pallas_call(
        functools.partial(pack_kernel, node_count),
        out_shape=jax.ShapeDtypeStruct((rows, 3 * channels), BF16),
        in_specs=[SMEM, SMEM, SMEM] + [VMEM] * utts,
        out_specs=VMEM,
        compiler_params=params(14),
        cost_estimate=cost(60 * 10**9, 160 * 10**6),
        name="pack",
    )(place, pair_table, dest_table, *arrived)
    steps = 4
    block = width // steps
    return pl.pallas_call(
        functools.partial(mix_kernel, node_count, offsets),
        out_shape=jax.ShapeDtypeStruct((pair_count, width), BF16),
        in_specs=[SMEM] * 3 + [VMEM] * 6 + [ANY],
        out_specs=VMEM,
        scratch_shapes=[
            pltpu.VMEM((3 * channels, channels), F32),
            pltpu.VMEM((channels, width), F32),
            pltpu.VMEM((rows, width), BF16),
            pltpu.VMEM((steps, 2, block, width), BF16),
            pltpu.VMEM((2, rows + 2 * GAP, block), F32),
            pltpu.VMEM((rows, width), F32),
            pltpu.SemaphoreType.DMA((steps,)),
        ],
        compiler_params=params(50),
        cost_estimate=cost(6 * 10**9, 14 * 10**6),
        name="mix",
    )(
        place,
        pair_table,
        dest_table,
        packed,
        mine,
        other,
        gain_first[None],
        depth_weight,
        gain_second[None],
        weight_full,
    )


def solution(mesh):
    in_specs = (
        P(("dp", "fsdp"), None),
        P("fsdp", None, None),
        P("fsdp", None, None),
        P("dp", None),
        P("dp", None),
        P(None, None, "fsdp"),
        P(),
        P(),
        P(),
    )
    out_specs = P(("dp", "fsdp"), None)
    return jax.shard_map(body, mesh=mesh, in_specs=in_specs, out_specs=out_specs, check_vma=False)
```

time: 139 us -> 120 us (0.86)
  blocking collectives: 14.5 us -> 0 us
  starting transfers between devices: 32.3 us -> 41.8 us
  waiting for transfers between devices: 38.1 us -> 29.1 us
  local copies, waits for them, and re-layouts: 8.04 us -> 3.63 us
    ppermute x6 -> x3, waiting for transfers between devices: 34.8 us -> 0.01 us  [shifted(): return lax.ppermute(value, axis, pairs)]
    ppermute x0 -> x4, waiting for transfers between devices: none -> 28.4 us  [along_z(): return lax.ppermute(value, 'dp', pairs)]
    ppermute x0 -> x4, starting transfers between devices: none -> 17.1 us  [along_z(): return lax.ppermute(value, 'dp', pairs)]
    all_to_all x1 -> x0, blocking collectives: 14.5 us -> none  [spread(): return lax.all_to_all(copies, axis, 0, 0, axis_index_groups=groups)]
    ppermute x6 -> x3, starting transfers between devices: 19.7 us -> 13.4 us  [shifted(): return lax.ppermute(value, axis, pairs)]
    ppermute x1, waiting for transfers between devices: 2.62 us -> 0.01 us  [core_swapped(): return lax.ppermute(value, axis, [(j, j ^ 1) for j in range(count)])]
    all_to_all x1, starting transfers between devices: 10 us -> 7.65 us  [body(): by_y = lax.all_to_all(copies, 'dp', 0, 0, axis_index_groups=y_groups)]
    unnamed x22 -> x26, local copies, waits for them, and re-layouts: 5.25 us -> 3.58 us
  transfers between devices with their start and end apart: 9 -> 10, of which waited for: 4 -> 4; matrix products, arithmetic and copies ran while one was open for 3% -> 0% of each run, Pallas kernels for 7% -> 7%
where the time goes in v2:
time: 120 us
  starting transfers between devices  41.8 us (35%)
  Pallas kernels  31.3 us (26%)
  waiting for transfers between devices  29.1 us (24%)
  between operations  13.7 us (11%)
  local copies, waits for them, and re-layouts  3.63 us (3%)
    ppermute x4, waiting for transfers between devices, along_z(): return lax.ppermute(value, 'dp', pairs)  28.4 us
    pallas_call x1, Pallas kernels, body(): pl.pallas_call(functools.partial(mix_kernel, node_count, offsets), out_sh...  22.9 us
    ppermute x4, starting transfers between devices, along_z(): return lax.ppermute(value, 'dp', pairs)  17.1 us
    ppermute x3, starting transfers between devices, shifted(): return lax.ppermute(value, axis, pairs)  13.4 us
    all_to_all x1, starting transfers between devices, body(): by_y = lax.all_to_all(copies, 'dp', 0, 0, axis_index_groups=y_groups)  7.65 us
    pallas_call x1, Pallas kernels, body(): pl.pallas_call(functools.partial(cut_kernel, node_count), out_shape=[jax....  3.78 us
    ppermute x1, starting transfers between devices, core_swapped(): return lax.ppermute(value, axis, [(j, j ^ 1) for j in range(count)])  3.64 us
    unnamed x26, local copies, waits for them, and re-layouts  3.58 us
  transfers between devices with their start and end apart: 10, of which 4 were waited for; matrix products, arithmetic and copies ran while one was open for 0% of the time, Pallas kernels for 7%

profile of v2, /device:TPU:1, one launch (start us, length us, event | category | flops | bytes accessed | tf_op | source)
XLA Modules:
  0.0 119.7 jit_solution(15822055720603648315)
XLA Ops:
  6.5 0.0 copy-start.5
  6.5 0.0 copy-start.4
  6.5 0.0 copy-start.2
  6.5 0.0 all-gather.2.cloned.1.call-start
  6.5 0.7 all-gather.2.cloned.1.call-update
  7.3 0.1 pad_add_fusion.place_ref
  7.3 0.0 copy-start
  7.3 0.7 copy-done
  8.1 0.0 copy-start.1
  8.1 0.7 copy-done.1
  8.8 1.3 %own.1 = bf16[8,24,512]{2,1,0:T(8,128)(2,1)} custom-call(s32[2]{0:T(128)S(1)} %pad_add_fusion.place_ref, bf16[24,512]{1,0:T(8,128)(2,1)S(1)} %copy-done, bf16[8,1536]{1,0:T(8,128)(2,1)S(1)} %copy-done.1), custom_call_target="tpu_custom_call" | custom-call | flops 100000 | bytes 300000 | tf_op jit(solution)/shard_map/own/pallas_call | solution.py:303
  10.1 7.7 %all-to-all-start = ((bf16[8,24,512]{2,1,0:T(8,128)(2,1)}), bf16[8,24,512]{2,1,0:T(8,128)(2,1)S(1)}, u32[]{:S(2)}, u32[]{:S(2)}) async-start(bf16[8,24,512]{2,1,0:T(8,128)(2,1)} %own.1), calls=%async_computation | async-start | bytes 393216 | tf_op jit(solution)/shard_map/all_to_all | solution.py:312
  17.7 0.0 copy-done.5
  17.7 0.0 copy-done.4
  17.7 0.0 copy-done.2
  17.7 0.0 copy-start.9
  17.8 0.0 copy-start.10
  17.8 3.8 %cut.1 = (bf16[256,1024]{1,0:T(8,128)(2,1)S(1)}, bf16[256,1024]{1,0:T(8,128)(2,1)}, bf16[256,1024]{1,0:T(8,128)(2,1)}, bf16[256,1024]{1,0:T(8,128)(2,1)}) custom-call(s32[2]{0:T(128)S(1)} %pad_add_fusion.place_ref, s32[4,64]{1,0:T(4,128)S(1)} %bitcast.15, s32[4,64]{1,0:T(4,128)S(1)} %bitcast.18, bf16[1024,512]{1,0:T(8,128)(2,1)S(1)} %copy-done.2), custom_call_target="tpu_custom_call" | custom-call | flops 4000000000 | bytes 4000000 | tf_op jit(solution)/shard_map/cut/pallas_call | solution.py:288
  21.6 0.0 copy-start.7
  21.6 0.8 copy-done.7
  22.4 7.3 %collective-permute-start.1 = (bf16[256,1024]{1,0:T(8,128)(2,1)}, bf16[256,1024]{1,0:T(8,128)(2,1)}, u32[]{:S(2)}, u32[]{:S(2)}) collective-permute-start(bf16[256,1024]{1,0:T(8,128)(2,1)} %get-tuple-element.12), channel_id=1, source_target_pairs={{0,256},{8,264},{16,272},{24,280},{32,288},{40,296},{48,304},{56,3... | collective-permute-start | bytes 1572872 | tf_op jit(solution)/shard_map/ppermute | solution.py:18
  29.6 2.2 %collective-permute-start.2 = (bf16[256,1024]{1,0:T(8,128)(2,1)}, bf16[256,1024]{1,0:T(8,128)(2,1)}, u32[]{:S(2)}, u32[]{:S(2)}) collective-permute-start(bf16[256,1024]{1,0:T(8,128)(2,1)} %get-tuple-element.13), channel_id=1, source_target_pairs={{0,384},{8,392},{16,400},{24,408},{32,416},{40,424},{48,432},{56,4... | collective-permute-start | bytes 1572872 | tf_op jit(solution)/shard_map/ppermute | solution.py:18
  31.8 4.0 %collective-permute-start = (bf16[256,1024]{1,0:T(8,128)(2,1)}, bf16[256,1024]{1,0:T(8,128)(2,1)}, u32[]{:S(2)}, u32[]{:S(2)}) collective-permute-start(bf16[256,1024]{1,0:T(8,128)(2,1)} %get-tuple-element.11), channel_id=1, source_target_pairs={{0,128},{8,136},{16,144},{24,152},{32,160},{40,168},{48,176},{56,1... | collective-permute-start | bytes 1572872 | tf_op jit(solution)/shard_map/ppermute | solution.py:18
  35.8 0.0 copy-done.9
  35.8 0.0 copy-done.10
  35.9 0.0 all-to-all-done
  35.9 10.6 %collective-permute-start.4 = (bf16[8,24,512]{2,1,0:T(8,128)(2,1)S(1)}, bf16[8,24,512]{2,1,0:T(8,128)(2,1)S(1)}, u32[]{:S(2)}, u32[]{:S(2)}) collective-permute-start(bf16[8,24,512]{2,1,0:T(8,128)(2,1)S(1)} %all-to-all-done), channel_id=1, source_target_pairs={{0,40},{8,48},{16,56},{24,0},{32,8},{40,16},{48,24},{56,32},{64,10... | collective-permute-start | bytes 589832 | tf_op jit(solution)/shard_map/ppermute | solution.py:30
  46.5 1.9 %collective-permute-start.3 = (bf16[8,24,512]{2,1,0:T(8,128)(2,1)S(1)}, bf16[8,24,512]{2,1,0:T(8,128)(2,1)S(1)}, u32[]{:S(2)}, u32[]{:S(2)}) collective-permute-start(bf16[8,24,512]{2,1,0:T(8,128)(2,1)S(1)} %all-to-all-done), channel_id=1, source_target_pairs={{0,24},{8,32},{16,40},{24,48},{32,56},{40,0},{48,8},{56,16},{64,88... | collective-permute-start | bytes 589832 | tf_op jit(solution)/shard_map/ppermute | solution.py:30
  48.5 9.6 %collective-permute-done.4 = bf16[8,24,512]{2,1,0:T(8,128)(2,1)S(1)} collective-permute-done((bf16[8,24,512]{2,1,0:T(8,128)(2,1)S(1)}, bf16[8,24,512]{2,1,0:T(8,128)(2,1)S(1)}, u32[]{:S(2)}, u32[]{:S(2)}) %collective-permute-start.4) | collective-permute-done | bytes 196640 | tf_op jit(solution)/shard_map/ppermute | solution.py:30
  58.1 2.5 %collective-permute-start.5 = (bf16[2,8,24,512]{3,2,1,0:T(8,128)(2,1)S(1)}, bf16[2,8,24,512]{3,2,1,0:T(8,128)(2,1)S(1)}, u32[]{:S(2)}, u32[]{:S(2)}) collective-permute-start(bf16[2,8,24,512]{3,2,1,0:T(8,128)(2,1)S(1)} %pad_maximum_fusion.1), channel_id=1, source_target_pairs={{0,8},{8,16},{16,24},{24,32},{32,40},{40,48},{48,56},{56,0},{64,72... | collective-permute-start | bytes 1179656 | tf_op jit(solution)/shard_map/ppermute | solution.py:30
  60.5 5.0 %collective-permute-done.3 = bf16[8,24,512]{2,1,0:T(8,128)(2,1)S(1)} collective-permute-done((bf16[8,24,512]{2,1,0:T(8,128)(2,1)S(1)}, bf16[8,24,512]{2,1,0:T(8,128)(2,1)S(1)}, u32[]{:S(2)}, u32[]{:S(2)}) %collective-permute-start.3) | collective-permute-done | bytes 196640 | tf_op jit(solution)/shard_map/ppermute | solution.py:30
  65.5 0.1 pad_maximum_fusion
  65.6 0.0 copy-start.8
  65.6 2.1 %collective-permute-start.6 = (bf16[3,8,24,512]{3,2,1,0:T(8,128)(2,1)S(1)}, bf16[3,8,24,512]{3,2,1,0:T(8,128)(2,1)S(1)}, u32[]{:S(2)}, u32[]{:S(2)}) collective-permute-start(bf16[3,8,24,512]{3,2,1,0:T(8,128)(2,1)S(1)} %pad_maximum_fusion), channel_id=1, source_target_pairs={{0,56},{8,0},{16,8},{24,16},{32,24},{40,32},{48,40},{56,48},{64,12... | collective-permute-start | bytes 1769480 | tf_op jit(solution)/shard_map/ppermute | solution.py:30
  67.7 6.9 %collective-permute-done.5 = bf16[2,8,24,512]{3,2,1,0:T(8,128)(2,1)S(1)} collective-permute-done((bf16[2,8,24,512]{3,2,1,0:T(8,128)(2,1)S(1)}, bf16[2,8,24,512]{3,2,1,0:T(8,128)(2,1)S(1)}, u32[]{:S(2)}, u32[]{:S(2)}) %collective-permute-start.5) | collective-permute-done | bytes 393248 | tf_op jit(solution)/shard_map/ppermute | solution.py:30
  74.6 7.0 %collective-permute-done.6 = bf16[3,8,24,512]{3,2,1,0:T(8,128)(2,1)S(1)} collective-permute-done((bf16[3,8,24,512]{3,2,1,0:T(8,128)(2,1)S(1)}, bf16[3,8,24,512]{3,2,1,0:T(8,128)(2,1)S(1)}, u32[]{:S(2)}, u32[]{:S(2)}) %collective-permute-start.6) | collective-permute-done | bytes 589856 | tf_op jit(solution)/shard_map/ppermute | solution.py:30
  81.7 3.6 %collective-permute-start.7 = (bf16[8,8,24,512]{3,2,1,0:T(8,128)(2,1)S(1)}, bf16[8,8,24,512]{3,2,1,0:T(8,128)(2,1)S(1)}, u32[]{:S(2)}, u32[]{:S(2)}) collective-permute-start(bf16[8,8,24,512]{3,2,1,0:T(8,128)(2,1)S(1)} %constant_dynamic-update-slice_fusion.mine_ref), channel_id=1, source_target_pairs={{0,1},{1,0},{2,3},{3,2},{4,5},{5,4},{6,7},{7,6},{8,9},{9,8},{10,11... | collective-permute-start | bytes 4718600 | tf_op jit(solution)/shard_map/ppermute | solution.py:23
  85.3 0.0 collective-permute-done.1.refs_2_
  85.3 0.0 collective-permute-done.2.refs_3_
  85.3 0.0 collective-permute-done.refs_1_
  85.3 0.0 copy-done.8
  85.4 0.0 copy-start.3
  85.4 3.4 %pack.1.xs_ref = bf16[560,1536]{1,0:T(8,128)(2,1)S(1)} custom-call(s32[2]{0:T(128)S(1)} %pad_add_fusion.place_ref, s32[4,64]{1,0:T(4,128)S(1)} %bitcast.16, s32[4,64]{1,0:T(4,128)S(1)} %bitcast.19, bf16[256,1024]{1,0:T(8,128)(2,1)S(1)} %copy-done.8, bf16[256,1024]{1,0:T(8,128)(2,1)} %collective-permute-done.refs_1_, ...), custom_call_target="tpu_custom_call" | custom-call | flops 60000002048 | bytes 160000000 | tf_op jit(solution)/shard_map/pack/pallas_call | solution.py:321
  88.8 0.0 copy-start.6
  88.8 1.2 copy-done.6
  90.0 0.0 collective-permute-done.7.other_ref
  90.0 0.0 all-gather.2.cloned.1.call-done.weight_ref
  90.0 0.0 copy-done.3
  90.0 22.9 %mix.1 = bf16[512,1536]{1,0:T(8,128)(2,1)} custom-call(s32[2]{0:T(128)S(1)} %pad_add_fusion.place_ref, s32[4,64]{1,0:T(4,128)S(1)} %bitcast.17, s32[4,64]{1,0:T(4,128)S(1)} %bitcast.20, bf16[560,1536]{1,0:T(8,128)(2,1)} %copy-done.6, bf16[8,8,24,512]{3,2,1,0:T(8,128)(2,1)S(1)} %constant_dynamic-update-slice_fusion.mine_ref, ...), custom_call_target="tpu_custom_call" | custom-call | flops 6000000000 | bytes 14000000 | tf_op jit(solution)/shard_map/mix/pallas_call | solution.py:332
  (8 shorter events, 0.2 us)
Async XLA Ops:
  6.5 11.2 %copy-start.5 = (s32[1,64,4]{1,2,0:T(4,128)S(1)}, s32[1,64,4]{1,2,0:T(4,128)}, u32[]{:S(2)}) copy-start(s32[1,64,4]{1,2,0:T(4,128)} %param.11) | copy-start | bytes 3076
  6.5 11.2 %copy-start.4 = (s32[1,64,4]{1,2,0:T(4,128)S(1)}, s32[1,64,4]{1,2,0:T(4,128)}, u32[]{:S(2)}) copy-start(s32[1,64,4]{1,2,0:T(4,128)} %param.10) | copy-start | bytes 3076
  6.5 11.2 %copy-start.2 = (bf16[1024,512]{1,0:T(8,128)(2,1)S(1)}, bf16[1024,512]{1,0:T(8,128)(2,1)}, u32[]{:S(2)}) copy-start(bf16[1024,512]{1,0:T(8,128)(2,1)} %frames_ref.1) | copy-start | bytes 3145732
  6.5 83.4 %all-gather.2.cloned.1.call-start = ((), (), s32[]{:S(2)}) async-start(), calls=%async_computation.1 | async-start | bytes 10616832 | tf_op jit(solution)/shard_map/all_gather | solution.py:286
  7.3 0.7 copy-start
  8.1 0.7 copy-start.1
  10.1 25.8 %all-to-all-start = ((bf16[8,24,512]{2,1,0:T(8,128)(2,1)}), bf16[8,24,512]{2,1,0:T(8,128)(2,1)S(1)}, u32[]{:S(2)}, u32[]{:S(2)}) async-start(bf16[8,24,512]{2,1,0:T(8,128)(2,1)} %own.1), calls=%async_computation | async-start | bytes 393216 | tf_op jit(solution)/shard_map/all_to_all | solution.py:312
  17.7 18.1 %copy-start.9 = (f32[1536]{0:T(1024)S(1)}, f32[1536]{0:T(1024)}, u32[]{:S(2)}) copy-start(f32[1536]{0:T(1024)} %param.16) | copy-start | bytes 18436
  17.8 18.1 %copy-start.10 = (f32[1536]{0:T(1024)S(1)}, f32[1536]{0:T(1024)}, u32[]{:S(2)}) copy-start(f32[1536]{0:T(1024)} %param.17) | copy-start | bytes 18436
  21.6 0.8 copy-start.7
  22.4 63.0 %collective-permute-start.1 = (bf16[256,1024]{1,0:T(8,128)(2,1)}, bf16[256,1024]{1,0:T(8,128)(2,1)}, u32[]{:S(2)}, u32[]{:S(2)}) collective-permute-start(bf16[256,1024]{1,0:T(8,128)(2,1)} %get-tuple-element.12), channel_id=1, source_target_pairs={{0,256},{8,264},{16,272},{24,280},{32,288},{40,296},{48,304},{56,3... | collective-permute-start | bytes 1572872 | tf_op jit(solution)/shard_map/ppermute | solution.py:18
  29.6 55.7 %collective-permute-start.2 = (bf16[256,1024]{1,0:T(8,128)(2,1)}, bf16[256,1024]{1,0:T(8,128)(2,1)}, u32[]{:S(2)}, u32[]{:S(2)}) collective-permute-start(bf16[256,1024]{1,0:T(8,128)(2,1)} %get-tuple-element.13), channel_id=1, source_target_pairs={{0,384},{8,392},{16,400},{24,408},{32,416},{40,424},{48,432},{56,4... | collective-permute-start | bytes 1572872 | tf_op jit(solution)/shard_map/ppermute | solution.py:18
  31.8 53.5 %collective-permute-start = (bf16[256,1024]{1,0:T(8,128)(2,1)}, bf16[256,1024]{1,0:T(8,128)(2,1)}, u32[]{:S(2)}, u32[]{:S(2)}) collective-permute-start(bf16[256,1024]{1,0:T(8,128)(2,1)} %get-tuple-element.11), channel_id=1, source_target_pairs={{0,128},{8,136},{16,144},{24,152},{32,160},{40,168},{48,176},{56,1... | collective-permute-start | bytes 1572872 | tf_op jit(solution)/shard_map/ppermute | solution.py:18
  35.9 22.2 %collective-permute-start.4 = (bf16[8,24,512]{2,1,0:T(8,128)(2,1)S(1)}, bf16[8,24,512]{2,1,0:T(8,128)(2,1)S(1)}, u32[]{:S(2)}, u32[]{:S(2)}) collective-permute-start(bf16[8,24,512]{2,1,0:T(8,128)(2,1)S(1)} %all-to-all-done), channel_id=1, source_target_pairs={{0,40},{8,48},{16,56},{24,0},{32,8},{40,16},{48,24},{56,32},{64,10... | collective-permute-start | bytes 589832 | tf_op jit(solution)/shard_map/ppermute | solution.py:30
  46.5 19.0 %collective-permute-start.3 = (bf16[8,24,512]{2,1,0:T(8,128)(2,1)S(1)}, bf16[8,24,512]{2,1,0:T(8,128)(2,1)S(1)}, u32[]{:S(2)}, u32[]{:S(2)}) collective-permute-start(bf16[8,24,512]{2,1,0:T(8,128)(2,1)S(1)} %all-to-all-done), channel_id=1, source_target_pairs={{0,24},{8,32},{16,40},{24,48},{32,56},{40,0},{48,8},{56,16},{64,88... | collective-permute-start | bytes 589832 | tf_op jit(solution)/shard_map/ppermute | solution.py:30
  58.1 16.5 %collective-permute-start.5 = (bf16[2,8,24,512]{3,2,1,0:T(8,128)(2,1)S(1)}, bf16[2,8,24,512]{3,2,1,0:T(8,128)(2,1)S(1)}, u32[]{:S(2)}, u32[]{:S(2)}) collective-permute-start(bf16[2,8,24,512]{3,2,1,0:T(8,128)(2,1)S(1)} %pad_maximum_fusion.1), channel_id=1, source_target_pairs={{0,8},{8,16},{16,24},{24,32},{32,40},{40,48},{48,56},{56,0},{64,72... | collective-permute-start | bytes 1179656 | tf_op jit(solution)/shard_map/ppermute | solution.py:30
  65.6 19.8 %copy-start.8 = (bf16[256,1024]{1,0:T(8,128)(2,1)S(1)}, bf16[256,1024]{1,0:T(8,128)(2,1)}, u32[]{:S(2)}) copy-start(bf16[256,1024]{1,0:T(8,128)(2,1)} %copy-done.7) | copy-start | bytes 1572868
  65.6 16.0 %collective-permute-start.6 = (bf16[3,8,24,512]{3,2,1,0:T(8,128)(2,1)S(1)}, bf16[3,8,24,512]{3,2,1,0:T(8,128)(2,1)S(1)}, u32[]{:S(2)}, u32[]{:S(2)}) collective-permute-start(bf16[3,8,24,512]{3,2,1,0:T(8,128)(2,1)S(1)} %pad_maximum_fusion), channel_id=1, source_target_pairs={{0,56},{8,0},{16,8},{24,16},{32,24},{40,32},{48,40},{56,48},{64,12... | collective-permute-start | bytes 1769480 | tf_op jit(solution)/shard_map/ppermute | solution.py:30
  81.7 8.3 %collective-permute-start.7 = (bf16[8,8,24,512]{3,2,1,0:T(8,128)(2,1)S(1)}, bf16[8,8,24,512]{3,2,1,0:T(8,128)(2,1)S(1)}, u32[]{:S(2)}, u32[]{:S(2)}) collective-permute-start(bf16[8,8,24,512]{3,2,1,0:T(8,128)(2,1)S(1)} %constant_dynamic-update-slice_fusion.mine_ref), channel_id=1, source_target_pairs={{0,1},{1,0},{2,3},{3,2},{4,5},{5,4},{6,7},{7,6},{8,9},{9,8},{10,11... | collective-permute-start | bytes 4718600 | tf_op jit(solution)/shard_map/ppermute | solution.py:23
  85.4 4.6 %copy-start.3 = (f32[31,1536]{1,0:T(8,128)S(1)}, f32[31,1536]{1,0:T(8,128)}, u32[]{:S(2)}) copy-start(f32[31,1536]{1,0:T(8,128)} %depth_ref.1) | copy-start | bytes 571396
  88.8 1.2 %copy-start.6 = (bf16[560,1536]{1,0:T(8,128)(2,1)}, bf16[560,1536]{1,0:T(8,128)(2,1)S(1)}, u32[]{:S(2)}) copy-start(bf16[560,1536]{1,0:T(8,128)(2,1)S(1)} %pack.1.xs_ref) | copy-start | bytes 5160964
Sparse Core Ops, SparseCore 0:
  9.5 65.3 all-gather.1

commit v3 on v2

--- a/solution.py
+++ b/solution.py
@@ -8,6 +8,7 @@
 from jax.sharding import PartitionSpec as P
 
 GAP = 16
+SUBLANES = 8
 BF16 = jnp.bfloat16
 F32 = jnp.float32
 
@@ -101,7 +102,9 @@
     channels = width // 2
     lengths, _, padded_starts = arriving(place_ref[0], pair_ref, dest_ref, node_count)
     shape = (rows, slot_rows)
-    behind = iota(shape, 0) - iota(shape, 1)
+    line = iota(shape, 0)
+    spread = (line & (SUBLANES - 1)) * (rows // SUBLANES) + (line >> 3)
+    behind = spread - iota(shape, 1)
     within = iota(shape, 1)
     both = jnp.zeros((rows, width), F32)
     earlier = jnp.zeros((rows, channels), F32)
@@ -150,26 +153,18 @@
 
 
 def depthwise(gated_ref, depth_ref, mixed_ref, lane, at):
-    rows = mixed_ref.shape[0]
     taps = depth_ref.shape[0]
-    span = 56
+    lines = mixed_ref.shape[0] // SUBLANES
     lanes = slice(lane, lane + 128)
-    for row in range(0, rows, span):
-        near = gated_ref[row : row + span + 32, lanes]
-        total = None
-        for low in range(7, -1, -1):
-            partial = None
-            for high in range(0, 32, 8):
-                tap = high + low - 1
-                if 0 <= tap < taps:
-                    weight = depth_ref[tap : tap + 1, at : at + 128]
-                    term = near[high : high + span + 8] * weight
-                    partial = term if partial is None else partial + term
-            if total is None:
-                total = partial
-            else:
-                total = partial + pltpu.roll(total, span + 7, 0)
-        mixed_ref[row : row + span, at : at + 128] = total[:span]
+    weights = [depth_ref[tap : tap + 1, at : at + 128] for tap in range(taps)]
+    span = 10
+    for line in range(0, lines, span):
+        near = gated_ref[line : line + span + taps - 1, :, lanes]
+        total = near[:span] * weights[0]
+        for tap in range(1, taps):
+            total += near[tap : tap + span] * weights[tap]
+        rows = slice(line * SUBLANES, (line + span) * SUBLANES)
+        mixed_ref[rows, at : at + 128] = total.reshape(span * SUBLANES, 128)
 
 
 def mix_kernel(
@@ -210,9 +205,9 @@
     projected = projected.astype(BF16).astype(F32)
     normed_ref[...] = layer_norm(projected, first_ref[...]).astype(BF16)
 
-    for buffer in range(2):
-        gated_ref[buffer, pl.ds(0, GAP), :] = jnp.zeros((GAP, block), F32)
-        gated_ref[buffer, pl.ds(GAP + rows, GAP), :] = jnp.zeros((GAP, block), F32)
+    lines = rows // SUBLANES
+    half = depth_ref.shape[0] // 2
+    edge = iota((half, SUBLANES, block), 1)
     contract = (((1,), (1,)), ((), ()))
 
     def multiply(step):
@@ -224,7 +219,13 @@
             for part in range(2)
         )
         gated = (value * jax.nn.sigmoid(gate)).astype(BF16)
-        gated_ref[step % 2, pl.ds(GAP, rows), :] = gated.astype(F32)
+        gated = gated.astype(F32).reshape(lines, SUBLANES, block)
+        before = pltpu.roll(gated[lines - half :], 1, 1)
+        after = pltpu.roll(gated[:half], SUBLANES - 1, 1)
+        held = gated_ref.at[step % 2]
+        held[:half] = jnp.where(edge > 0, before, 0.0)
+        held[half : half + lines] = gated
+        held[half + lines :] = jnp.where(edge < SUBLANES - 1, after, 0.0)
 
     multiply(0)
     for step in range(steps):
@@ -236,12 +237,15 @@
     scaled = layer_norm(mixed_ref[...], gain_ref[...])
     encoded = (scaled * jax.nn.sigmoid(scaled)).astype(BF16)
     _, starts, _ = arriving(place_ref[0], pair_ref, dest_ref, node_count)
-    shape = (out_ref.shape[0], rows)
-    row_ids = iota(shape, 0)
+    row_ids = iota((out_ref.shape[0], 1), 0)
     target = row_ids - GAP
     for start in starts:
         target += jnp.where(row_ids >= start, GAP, 0)
-    chosen = as_bf16(iota(shape, 1) == target)
+    sublane = jnp.zeros_like(target)
+    for turn in range(1, SUBLANES):
+        sublane += jnp.where(target >= turn * lines, 1, 0)
+    target = (target - sublane * lines) * SUBLANES + sublane
+    chosen = as_bf16(iota((out_ref.shape[0], rows), 1) == target)
     out_ref[...] = jnp.dot(chosen, encoded, preferred_element_type=F32).astype(BF16)
 
 
@@ -327,7 +331,7 @@
         cost_estimate=cost(60 * 10**9, 160 * 10**6),
         name="pack",
     )(place, pair_table, dest_table, *arrived)
-    steps = 4
+    steps = 6
     block = width // steps
     return pl.pallas_call(
         functools.partial(mix_kernel, node_count, offsets),
@@ -339,7 +343,7 @@
             pltpu.VMEM((channels, width), F32),
             pltpu.VMEM((rows, width), BF16),
             pltpu.VMEM((steps, 2, block, width), BF16),
-            pltpu.VMEM((2, rows + 2 * GAP, block), F32),
+            pltpu.VMEM((2, rows // SUBLANES + depth_weight.shape[0] - 1, SUBLANES, block), F32),
             pltpu.VMEM((rows, width), F32),
             pltpu.SemaphoreType.DMA((steps,)),
         ],

time: 120 us -> 117 us (0.975)
  Pallas kernels: 31.3 us -> 28.4 us
    pallas_call x1, Pallas kernels: 22.9 us -> 20 us  [body(): pl.pallas_call(functools.partial(mix_kernel, node_count, offsets), out_sh...]
where the time goes in v3:
time: 117 us
  starting transfers between devices  41.8 us (36%)
  waiting for transfers between devices  29.1 us (25%)
  Pallas kernels  28.4 us (24%)
  between operations  13.7 us (12%)
  local copies, waits for them, and re-layouts  3.63 us (3%)
    ppermute x4, waiting for transfers between devices, along_z(): return lax.ppermute(value, 'dp', pairs)  28.4 us
    pallas_call x1, Pallas kernels, body(): pl.pallas_call(functools.partial(mix_kernel, node_count, offsets), out_sh...  20 us
    ppermute x4, starting transfers between devices, along_z(): return lax.ppermute(value, 'dp', pairs)  17.1 us
    ppermute x3, starting transfers between devices, shifted(): return lax.ppermute(value, axis, pairs)  13.4 us
    all_to_all x1, starting transfers between devices, body(): by_y = lax.all_to_all(copies, 'dp', 0, 0, axis_index_groups=y_groups)  7.65 us
    pallas_call x1, Pallas kernels, body(): pl.pallas_call(functools.partial(cut_kernel, node_count), out_shape=[jax....  3.78 us
    ppermute x1, starting transfers between devices, core_swapped(): return lax.ppermute(value, axis, [(j, j ^ 1) for j in range(count)])  3.64 us
    unnamed x26, local copies, waits for them, and re-layouts  3.58 us
  transfers between devices with their start and end apart: 10, of which 4 were waited for; matrix products, arithmetic and copies ran while one was open for 0% of the time, Pallas kernels for 7%

profile of v3, /device:TPU:1, one launch (start us, length us, event | category | flops | bytes accessed | tf_op | source)
XLA Modules:
  0.0 116.8 jit_solution(2819918173175381699)
XLA Ops:
  6.5 0.0 copy-start.5
  6.5 0.0 copy-start.4
  6.5 0.0 copy-start.2
  6.5 0.0 all-gather.2.cloned.1.call-start
  6.5 0.7 all-gather.2.cloned.1.call-update
  7.3 0.1 pad_add_fusion.place_ref
  7.3 0.0 copy-start
  7.3 0.7 copy-done
  8.1 0.0 copy-start.1
  8.1 0.7 copy-done.1
  8.8 1.3 %own.1 = bf16[8,24,512]{2,1,0:T(8,128)(2,1)} custom-call(s32[2]{0:T(128)S(1)} %pad_add_fusion.place_ref, bf16[24,512]{1,0:T(8,128)(2,1)S(1)} %copy-done, bf16[8,1536]{1,0:T(8,128)(2,1)S(1)} %copy-done.1), custom_call_target="tpu_custom_call" | custom-call | flops 100000 | bytes 300000 | tf_op jit(solution)/shard_map/own/pallas_call | solution.py:307
  10.1 7.7 %all-to-all-start = ((bf16[8,24,512]{2,1,0:T(8,128)(2,1)}), bf16[8,24,512]{2,1,0:T(8,128)(2,1)S(1)}, u32[]{:S(2)}, u32[]{:S(2)}) async-start(bf16[8,24,512]{2,1,0:T(8,128)(2,1)} %own.1), calls=%async_computation | async-start | bytes 393216 | tf_op jit(solution)/shard_map/all_to_all | solution.py:316
  17.7 0.0 copy-done.5
  17.7 0.0 copy-done.4
  17.7 0.0 copy-done.2
  17.7 0.0 copy-start.9
  17.8 0.0 copy-start.10
  17.8 3.8 %cut.1 = (bf16[256,1024]{1,0:T(8,128)(2,1)S(1)}, bf16[256,1024]{1,0:T(8,128)(2,1)}, bf16[256,1024]{1,0:T(8,128)(2,1)}, bf16[256,1024]{1,0:T(8,128)(2,1)}) custom-call(s32[2]{0:T(128)S(1)} %pad_add_fusion.place_ref, s32[4,64]{1,0:T(4,128)S(1)} %bitcast.15, s32[4,64]{1,0:T(4,128)S(1)} %bitcast.18, bf16[1024,512]{1,0:T(8,128)(2,1)S(1)} %copy-done.2), custom_call_target="tpu_custom_call" | custom-call | flops 4000000000 | bytes 4000000 | tf_op jit(solution)/shard_map/cut/pallas_call | solution.py:292
  21.6 0.0 copy-start.7
  21.6 0.8 copy-done.7
  22.4 7.3 %collective-permute-start.1 = (bf16[256,1024]{1,0:T(8,128)(2,1)}, bf16[256,1024]{1,0:T(8,128)(2,1)}, u32[]{:S(2)}, u32[]{:S(2)}) collective-permute-start(bf16[256,1024]{1,0:T(8,128)(2,1)} %get-tuple-element.12), channel_id=1, source_target_pairs={{0,256},{8,264},{16,272},{24,280},{32,288},{40,296},{48,304},{56,3... | collective-permute-start | bytes 1572872 | tf_op jit(solution)/shard_map/ppermute | solution.py:19
  29.6 2.2 %collective-permute-start.2 = (bf16[256,1024]{1,0:T(8,128)(2,1)}, bf16[256,1024]{1,0:T(8,128)(2,1)}, u32[]{:S(2)}, u32[]{:S(2)}) collective-permute-start(bf16[256,1024]{1,0:T(8,128)(2,1)} %get-tuple-element.13), channel_id=1, source_target_pairs={{0,384},{8,392},{16,400},{24,408},{32,416},{40,424},{48,432},{56,4... | collective-permute-start | bytes 1572872 | tf_op jit(solution)/shard_map/ppermute | solution.py:19
  31.8 4.0 %collective-permute-start = (bf16[256,1024]{1,0:T(8,128)(2,1)}, bf16[256,1024]{1,0:T(8,128)(2,1)}, u32[]{:S(2)}, u32[]{:S(2)}) collective-permute-start(bf16[256,1024]{1,0:T(8,128)(2,1)} %get-tuple-element.11), channel_id=1, source_target_pairs={{0,128},{8,136},{16,144},{24,152},{32,160},{40,168},{48,176},{56,1... | collective-permute-start | bytes 1572872 | tf_op jit(solution)/shard_map/ppermute | solution.py:19
  35.8 0.0 copy-done.9
  35.8 0.0 copy-done.10
  35.9 0.0 all-to-all-done
  35.9 10.6 %collective-permute-start.4 = (bf16[8,24,512]{2,1,0:T(8,128)(2,1)S(1)}, bf16[8,24,512]{2,1,0:T(8,128)(2,1)S(1)}, u32[]{:S(2)}, u32[]{:S(2)}) collective-permute-start(bf16[8,24,512]{2,1,0:T(8,128)(2,1)S(1)} %all-to-all-done), channel_id=1, source_target_pairs={{0,40},{8,48},{16,56},{24,0},{32,8},{40,16},{48,24},{56,32},{64,10... | collective-permute-start | bytes 589832 | tf_op jit(solution)/shard_map/ppermute | solution.py:31
  46.5 1.9 %collective-permute-start.3 = (bf16[8,24,512]{2,1,0:T(8,128)(2,1)S(1)}, bf16[8,24,512]{2,1,0:T(8,128)(2,1)S(1)}, u32[]{:S(2)}, u32[]{:S(2)}) collective-permute-start(bf16[8,24,512]{2,1,0:T(8,128)(2,1)S(1)} %all-to-all-done), channel_id=1, source_target_pairs={{0,24},{8,32},{16,40},{24,48},{32,56},{40,0},{48,8},{56,16},{64,88... | collective-permute-start | bytes 589832 | tf_op jit(solution)/shard_map/ppermute | solution.py:31
  48.5 9.6 %collective-permute-done.4 = bf16[8,24,512]{2,1,0:T(8,128)(2,1)S(1)} collective-permute-done((bf16[8,24,512]{2,1,0:T(8,128)(2,1)S(1)}, bf16[8,24,512]{2,1,0:T(8,128)(2,1)S(1)}, u32[]{:S(2)}, u32[]{:S(2)}) %collective-permute-start.4) | collective-permute-done | bytes 196640 | tf_op jit(solution)/shard_map/ppermute | solution.py:31
  58.1 2.5 %collective-permute-start.5 = (bf16[2,8,24,512]{3,2,1,0:T(8,128)(2,1)S(1)}, bf16[2,8,24,512]{3,2,1,0:T(8,128)(2,1)S(1)}, u32[]{:S(2)}, u32[]{:S(2)}) collective-permute-start(bf16[2,8,24,512]{3,2,1,0:T(8,128)(2,1)S(1)} %pad_maximum_fusion.1), channel_id=1, source_target_pairs={{0,8},{8,16},{16,24},{24,32},{32,40},{40,48},{48,56},{56,0},{64,72... | collective-permute-start | bytes 1179656 | tf_op jit(solution)/shard_map/ppermute | solution.py:31
  60.5 5.0 %collective-permute-done.3 = bf16[8,24,512]{2,1,0:T(8,128)(2,1)S(1)} collective-permute-done((bf16[8,24,512]{2,1,0:T(8,128)(2,1)S(1)}, bf16[8,24,512]{2,1,0:T(8,128)(2,1)S(1)}, u32[]{:S(2)}, u32[]{:S(2)}) %collective-permute-start.3) | collective-permute-done | bytes 196640 | tf_op jit(solution)/shard_map/ppermute | solution.py:31
  65.5 0.1 pad_maximum_fusion
  65.6 0.0 copy-start.8
  65.6 2.1 %collective-permute-start.6 = (bf16[3,8,24,512]{3,2,1,0:T(8,128)(2,1)S(1)}, bf16[3,8,24,512]{3,2,1,0:T(8,128)(2,1)S(1)}, u32[]{:S(2)}, u32[]{:S(2)}) collective-permute-start(bf16[3,8,24,512]{3,2,1,0:T(8,128)(2,1)S(1)} %pad_maximum_fusion), channel_id=1, source_target_pairs={{0,56},{8,0},{16,8},{24,16},{32,24},{40,32},{48,40},{56,48},{64,12... | collective-permute-start | bytes 1769480 | tf_op jit(solution)/shard_map/ppermute | solution.py:31
  67.7 6.9 %collective-permute-done.5 = bf16[2,8,24,512]{3,2,1,0:T(8,128)(2,1)S(1)} collective-permute-done((bf16[2,8,24,512]{3,2,1,0:T(8,128)(2,1)S(1)}, bf16[2,8,24,512]{3,2,1,0:T(8,128)(2,1)S(1)}, u32[]{:S(2)}, u32[]{:S(2)}) %collective-permute-start.5) | collective-permute-done | bytes 393248 | tf_op jit(solution)/shard_map/ppermute | solution.py:31
  74.6 7.0 %collective-permute-done.6 = bf16[3,8,24,512]{3,2,1,0:T(8,128)(2,1)S(1)} collective-permute-done((bf16[3,8,24,512]{3,2,1,0:T(8,128)(2,1)S(1)}, bf16[3,8,24,512]{3,2,1,0:T(8,128)(2,1)S(1)}, u32[]{:S(2)}, u32[]{:S(2)}) %collective-permute-start.6) | collective-permute-done | bytes 589856 | tf_op jit(solution)/shard_map/ppermute | solution.py:31
  81.7 3.6 %collective-permute-start.7 = (bf16[8,8,24,512]{3,2,1,0:T(8,128)(2,1)S(1)}, bf16[8,8,24,512]{3,2,1,0:T(8,128)(2,1)S(1)}, u32[]{:S(2)}, u32[]{:S(2)}) collective-permute-start(bf16[8,8,24,512]{3,2,1,0:T(8,128)(2,1)S(1)} %constant_dynamic-update-slice_fusion.mine_ref), channel_id=1, source_target_pairs={{0,1},{1,0},{2,3},{3,2},{4,5},{5,4},{6,7},{7,6},{8,9},{9,8},{10,11... | collective-permute-start | bytes 4718600 | tf_op jit(solution)/shard_map/ppermute | solution.py:24
  85.3 0.0 collective-permute-done.1.refs_2_
  85.3 0.0 collective-permute-done.2.refs_3_
  85.3 0.0 collective-permute-done.refs_1_
  85.3 0.0 copy-done.8
  85.4 0.0 copy-start.3
  85.4 3.4 %pack.1.xs_ref = bf16[560,1536]{1,0:T(8,128)(2,1)S(1)} custom-call(s32[2]{0:T(128)S(1)} %pad_add_fusion.place_ref, s32[4,64]{1,0:T(4,128)S(1)} %bitcast.16, s32[4,64]{1,0:T(4,128)S(1)} %bitcast.19, bf16[256,1024]{1,0:T(8,128)(2,1)S(1)} %copy-done.8, bf16[256,1024]{1,0:T(8,128)(2,1)} %collective-permute-done.refs_1_, ...), custom_call_target="tpu_custom_call" | custom-call | flops 60000002048 | bytes 160000000 | tf_op jit(solution)/shard_map/pack/pallas_call | solution.py:325
  88.8 0.0 copy-start.6
  88.8 1.2 %copy-done.6 = bf16[560,1536]{1,0:T(8,128)(2,1)} copy-done((bf16[560,1536]{1,0:T(8,128)(2,1)}, bf16[560,1536]{1,0:T(8,128)(2,1)S(1)}, u32[]{:S(2)}) %copy-start.6) | copy-done | bytes 1720344
  90.0 0.0 collective-permute-done.7.other_ref
  90.0 0.0 all-gather.2.cloned.1.call-done.weight_ref
  90.0 0.0 copy-done.3
  90.0 20.0 %mix.1 = bf16[512,1536]{1,0:T(8,128)(2,1)} custom-call(s32[2]{0:T(128)S(1)} %pad_add_fusion.place_ref, s32[4,64]{1,0:T(4,128)S(1)} %bitcast.17, s32[4,64]{1,0:T(4,128)S(1)} %bitcast.20, bf16[560,1536]{1,0:T(8,128)(2,1)} %copy-done.6, bf16[8,8,24,512]{3,2,1,0:T(8,128)(2,1)S(1)} %constant_dynamic-update-slice_fusion.mine_ref, ...), custom_call_target="tpu_custom_call" | custom-call | flops 6000000000 | bytes 14000000 | tf_op jit(solution)/shard_map/mix/pallas_call | solution.py:336
  (8 shorter events, 0.2 us)
Async XLA Ops:
  6.5 11.2 %copy-start.5 = (s32[1,64,4]{1,2,0:T(4,128)S(1)}, s32[1,64,4]{1,2,0:T(4,128)}, u32[]{:S(2)}) copy-start(s32[1,64,4]{1,2,0:T(4,128)} %param.11) | copy-start | bytes 3076
  6.5 11.2 %copy-start.4 = (s32[1,64,4]{1,2,0:T(4,128)S(1)}, s32[1,64,4]{1,2,0:T(4,128)}, u32[]{:S(2)}) copy-start(s32[1,64,4]{1,2,0:T(4,128)} %param.10) | copy-start | bytes 3076
  6.5 11.2 %copy-start.2 = (bf16[1024,512]{1,0:T(8,128)(2,1)S(1)}, bf16[1024,512]{1,0:T(8,128)(2,1)}, u32[]{:S(2)}) copy-start(bf16[1024,512]{1,0:T(8,128)(2,1)} %frames_ref.1) | copy-start | bytes 3145732
  6.5 83.4 %all-gather.2.cloned.1.call-start = ((), (), s32[]{:S(2)}) async-start(), calls=%async_computation.1 | async-start | bytes 10616832 | tf_op jit(solution)/shard_map/all_gather | solution.py:290
  7.3 0.7 copy-start
  8.1 0.7 copy-start.1
  10.1 25.8 %all-to-all-start = ((bf16[8,24,512]{2,1,0:T(8,128)(2,1)}), bf16[8,24,512]{2,1,0:T(8,128)(2,1)S(1)}, u32[]{:S(2)}, u32[]{:S(2)}) async-start(bf16[8,24,512]{2,1,0:T(8,128)(2,1)} %own.1), calls=%async_computation | async-start | bytes 393216 | tf_op jit(solution)/shard_map/all_to_all | solution.py:316
  17.7 18.1 %copy-start.9 = (f32[1536]{0:T(1024)S(1)}, f32[1536]{0:T(1024)}, u32[]{:S(2)}) copy-start(f32[1536]{0:T(1024)} %param.16) | copy-start | bytes 18436
  17.8 18.1 %copy-start.10 = (f32[1536]{0:T(1024)S(1)}, f32[1536]{0:T(1024)}, u32[]{:S(2)}) copy-start(f32[1536]{0:T(1024)} %param.17) | copy-start | bytes 18436
  21.6 0.8 copy-start.7
  22.4 63.0 %collective-permute-start.1 = (bf16[256,1024]{1,0:T(8,128)(2,1)}, bf16[256,1024]{1,0:T(8,128)(2,1)}, u32[]{:S(2)}, u32[]{:S(2)}) collective-permute-start(bf16[256,1024]{1,0:T(8,128)(2,1)} %get-tuple-element.12), channel_id=1, source_target_pairs={{0,256},{8,264},{16,272},{24,280},{32,288},{40,296},{48,304},{56,3... | collective-permute-start | bytes 1572872 | tf_op jit(solution)/shard_map/ppermute | solution.py:19
  29.6 55.7 %collective-permute-start.2 = (bf16[256,1024]{1,0:T(8,128)(2,1)}, bf16[256,1024]{1,0:T(8,128)(2,1)}, u32[]{:S(2)}, u32[]{:S(2)}) collective-permute-start(bf16[256,1024]{1,0:T(8,128)(2,1)} %get-tuple-element.13), channel_id=1, source_target_pairs={{0,384},{8,392},{16,400},{24,408},{32,416},{40,424},{48,432},{56,4... | collective-permute-start | bytes 1572872 | tf_op jit(solution)/shard_map/ppermute | solution.py:19
  31.8 53.5 %collective-permute-start = (bf16[256,1024]{1,0:T(8,128)(2,1)}, bf16[256,1024]{1,0:T(8,128)(2,1)}, u32[]{:S(2)}, u32[]{:S(2)}) collective-permute-start(bf16[256,1024]{1,0:T(8,128)(2,1)} %get-tuple-element.11), channel_id=1, source_target_pairs={{0,128},{8,136},{16,144},{24,152},{32,160},{40,168},{48,176},{56,1... | collective-permute-start | bytes 1572872 | tf_op jit(solution)/shard_map/ppermute | solution.py:19
  35.9 22.2 %collective-permute-start.4 = (bf16[8,24,512]{2,1,0:T(8,128)(2,1)S(1)}, bf16[8,24,512]{2,1,0:T(8,128)(2,1)S(1)}, u32[]{:S(2)}, u32[]{:S(2)}) collective-permute-start(bf16[8,24,512]{2,1,0:T(8,128)(2,1)S(1)} %all-to-all-done), channel_id=1, source_target_pairs={{0,40},{8,48},{16,56},{24,0},{32,8},{40,16},{48,24},{56,32},{64,10... | collective-permute-start | bytes 589832 | tf_op jit(solution)/shard_map/ppermute | solution.py:31
  46.5 19.0 %collective-permute-start.3 = (bf16[8,24,512]{2,1,0:T(8,128)(2,1)S(1)}, bf16[8,24,512]{2,1,0:T(8,128)(2,1)S(1)}, u32[]{:S(2)}, u32[]{:S(2)}) collective-permute-start(bf16[8,24,512]{2,1,0:T(8,128)(2,1)S(1)} %all-to-all-done), channel_id=1, source_target_pairs={{0,24},{8,32},{16,40},{24,48},{32,56},{40,0},{48,8},{56,16},{64,88... | collective-permute-start | bytes 589832 | tf_op jit(solution)/shard_map/ppermute | solution.py:31
  58.1 16.5 %collective-permute-start.5 = (bf16[2,8,24,512]{3,2,1,0:T(8,128)(2,1)S(1)}, bf16[2,8,24,512]{3,2,1,0:T(8,128)(2,1)S(1)}, u32[]{:S(2)}, u32[]{:S(2)}) collective-permute-start(bf16[2,8,24,512]{3,2,1,0:T(8,128)(2,1)S(1)} %pad_maximum_fusion.1), channel_id=1, source_target_pairs={{0,8},{8,16},{16,24},{24,32},{32,40},{40,48},{48,56},{56,0},{64,72... | collective-permute-start | bytes 1179656 | tf_op jit(solution)/shard_map/ppermute | solution.py:31
  65.6 19.8 %copy-start.8 = (bf16[256,1024]{1,0:T(8,128)(2,1)S(1)}, bf16[256,1024]{1,0:T(8,128)(2,1)}, u32[]{:S(2)}) copy-start(bf16[256,1024]{1,0:T(8,128)(2,1)} %copy-done.7) | copy-start | bytes 1572868
  65.6 16.0 %collective-permute-start.6 = (bf16[3,8,24,512]{3,2,1,0:T(8,128)(2,1)S(1)}, bf16[3,8,24,512]{3,2,1,0:T(8,128)(2,1)S(1)}, u32[]{:S(2)}, u32[]{:S(2)}) collective-permute-start(bf16[3,8,24,512]{3,2,1,0:T(8,128)(2,1)S(1)} %pad_maximum_fusion), channel_id=1, source_target_pairs={{0,56},{8,0},{16,8},{24,16},{32,24},{40,32},{48,40},{56,48},{64,12... | collective-permute-start | bytes 1769480 | tf_op jit(solution)/shard_map/ppermute | solution.py:31
  81.7 8.3 %collective-permute-start.7 = (bf16[8,8,24,512]{3,2,1,0:T(8,128)(2,1)S(1)}, bf16[8,8,24,512]{3,2,1,0:T(8,128)(2,1)S(1)}, u32[]{:S(2)}, u32[]{:S(2)}) collective-permute-start(bf16[8,8,24,512]{3,2,1,0:T(8,128)(2,1)S(1)} %constant_dynamic-update-slice_fusion.mine_ref), channel_id=1, source_target_pairs={{0,1},{1,0},{2,3},{3,2},{4,5},{5,4},{6,7},{7,6},{8,9},{9,8},{10,11... | collective-permute-start | bytes 4718600 | tf_op jit(solution)/shard_map/ppermute | solution.py:24
  85.4 4.6 %copy-start.3 = (f32[31,1536]{1,0:T(8,128)S(1)}, f32[31,1536]{1,0:T(8,128)}, u32[]{:S(2)}) copy-start(f32[31,1536]{1,0:T(8,128)} %depth_ref.1) | copy-start | bytes 571396
  88.8 1.2 %copy-start.6 = (bf16[560,1536]{1,0:T(8,128)(2,1)}, bf16[560,1536]{1,0:T(8,128)(2,1)S(1)}, u32[]{:S(2)}) copy-start(bf16[560,1536]{1,0:T(8,128)(2,1)S(1)} %pack.1.xs_ref) | copy-start | bytes 5160964
Sparse Core Ops, SparseCore 0:
  9.5 65.3 all-gather.1

commit v4 on v3

--- a/solution.py
+++ b/solution.py
@@ -86,12 +86,15 @@
             target = lax.rem(own + slot * spacing, node_count)
             starts[slot] += jnp.where(dest_ref[utt, own] == target, offset, 0)
         offset += pair_ref[utt, own]
-    shape = (slot_rows, frame_count)
+    window = 2 * slot_rows + 16
+    shape = (slot_rows, window)
     ahead = iota(shape, 1) - 2 * iota(shape, 0)
     for slot in range(utts):
+        base = jnp.minimum((2 * starts[slot]) // 16 * 16, frame_count - window)
+        near = frames_ref[pl.ds(pl.multiple_of(base, 16), window), :]
         for parity in range(2):
-            chosen = as_bf16(ahead == 2 * starts[slot] + parity)
-            rows = jnp.dot(chosen, frames_ref[...], preferred_element_type=F32)
+            chosen = as_bf16(ahead == 2 * starts[slot] - base + parity)
+            rows = jnp.dot(chosen, near, preferred_element_type=F32)
             out_refs[slot][:, parity * channels : (parity + 1) * channels] = rows.astype(BF16)
 
 
@@ -106,13 +109,21 @@
     spread = (line & (SUBLANES - 1)) * (rows // SUBLANES) + (line >> 3)
     behind = spread - iota(shape, 1)
     within = iota(shape, 1)
+    lines = rows // SUBLANES
+    place = iota((rows, 1), 0)
+    place = (place & (SUBLANES - 1)) * lines + (place >> 3)
     both = jnp.zeros((rows, width), F32)
-    earlier = jnp.zeros((rows, channels), F32)
+    filled = jnp.zeros((rows, 1), F32)
     for slot, piece_ref in enumerate(piece_refs):
         here = as_bf16((behind == padded_starts[slot]) & (within < lengths[slot]))
         both += jnp.dot(here, piece_ref[...], preferred_element_type=F32)
-        later = as_bf16((behind == padded_starts[slot] + 1) & (within < lengths[slot] - 1))
-        earlier += jnp.dot(later, piece_ref[:, channels:], preferred_element_type=F32)
+        since = place - padded_starts[slot]
+        filled += jnp.where((since >= 0) & (since < lengths[slot]), 1.0, 0.0)
+    odd = both[:, channels:].reshape(lines, SUBLANES, channels)
+    first = pltpu.roll(odd[lines - 1 :], 1, 1)
+    first = jnp.where(iota(first.shape, 1) > 0, first, 0.0)
+    earlier = jnp.concatenate([first, odd[:-1]], axis=0).reshape(rows, channels)
+    earlier = jnp.where(filled > 0.0, earlier, 0.0)
     out_ref[:, :channels] = earlier.astype(BF16)
     out_ref[:, channels:] = both.astype(BF16)
 

time: 117 us -> 116 us (level)
  transfers between devices with their start and end apart: 10 -> 10, of which waited for: 4 -> 4; matrix products, arithmetic and copies ran while one was open for 0% -> 0% of each run, Pallas kernels for 7% -> 6%
where the time goes in v4:
time: 116 us
  starting transfers between devices  41.8 us (36%)
  waiting for transfers between devices  29.1 us (25%)
  Pallas kernels  27.4 us (24%)
  between operations  13.7 us (12%)
  local copies, waits for them, and re-layouts  3.63 us (3%)
    ppermute x4, waiting for transfers between devices, along_z(): return lax.ppermute(value, 'dp', pairs)  28.4 us
    pallas_call x1, Pallas kernels, body(): pl.pallas_call(functools.partial(mix_kernel, node_count, offsets), out_sh...  20 us
    ppermute x4, starting transfers between devices, along_z(): return lax.ppermute(value, 'dp', pairs)  17.1 us
    ppermute x3, starting transfers between devices, shifted(): return lax.ppermute(value, axis, pairs)  13.4 us
    all_to_all x1, starting transfers between devices, body(): by_y = lax.all_to_all(copies, 'dp', 0, 0, axis_index_groups=y_groups)  7.65 us
    ppermute x1, starting transfers between devices, core_swapped(): return lax.ppermute(value, axis, [(j, j ^ 1) for j in range(count)])  3.63 us
    unnamed x26, local copies, waits for them, and re-layouts  3.58 us
    pallas_call x1, Pallas kernels, body(): pl.pallas_call(functools.partial(cut_kernel, node_count), out_shape=[jax....  3.27 us
  transfers between devices with their start and end apart: 10, of which 4 were waited for; matrix products, arithmetic and copies ran while one was open for 0% of the time, Pallas kernels for 6%

profile of v4, /device:TPU:1, one launch (start us, length us, event | category | flops | bytes accessed | tf_op | source)
XLA Modules:
  0.0 115.8 jit_solution(6532429005052294843)
XLA Ops:
  6.5 0.0 copy-start.5
  6.5 0.0 copy-start.4
  6.5 0.0 copy-start.2
  6.5 0.0 all-gather.2.cloned.1.call-start
  6.5 0.7 all-gather.2.cloned.1.call-update
  7.3 0.1 pad_add_fusion.place_ref
  7.3 0.0 copy-start
  7.3 0.7 copy-done
  8.1 0.0 copy-start.1
  8.1 0.7 copy-done.1
  8.8 1.3 %own.1 = bf16[8,24,512]{2,1,0:T(8,128)(2,1)} custom-call(s32[2]{0:T(128)S(1)} %pad_add_fusion.place_ref, bf16[24,512]{1,0:T(8,128)(2,1)S(1)} %copy-done, bf16[8,1536]{1,0:T(8,128)(2,1)S(1)} %copy-done.1), custom_call_target="tpu_custom_call" | custom-call | flops 100000 | bytes 300000 | tf_op jit(solution)/shard_map/own/pallas_call | solution.py:318
  10.1 7.7 %all-to-all-start = ((bf16[8,24,512]{2,1,0:T(8,128)(2,1)}), bf16[8,24,512]{2,1,0:T(8,128)(2,1)S(1)}, u32[]{:S(2)}, u32[]{:S(2)}) async-start(bf16[8,24,512]{2,1,0:T(8,128)(2,1)} %own.1), calls=%async_computation | async-start | bytes 393216 | tf_op jit(solution)/shard_map/all_to_all | solution.py:327
  17.7 0.0 copy-done.5
  17.7 0.0 copy-done.4
  17.7 0.0 copy-done.2
  17.7 0.0 copy-start.9
  17.8 0.0 copy-start.10
  17.8 3.3 %cut.1 = (bf16[256,1024]{1,0:T(8,128)(2,1)S(1)}, bf16[256,1024]{1,0:T(8,128)(2,1)}, bf16[256,1024]{1,0:T(8,128)(2,1)}, bf16[256,1024]{1,0:T(8,128)(2,1)}) custom-call(s32[2]{0:T(128)S(1)} %pad_add_fusion.place_ref, s32[4,64]{1,0:T(4,128)S(1)} %bitcast.15, s32[4,64]{1,0:T(4,128)S(1)} %bitcast.18, bf16[1024,512]{1,0:T(8,128)(2,1)S(1)} %copy-done.2), custom_call_target="tpu_custom_call" | custom-call | flops 4000000000 | bytes 4000000 | tf_op jit(solution)/shard_map/cut/pallas_call | solution.py:303
  21.0 0.0 copy-start.7
  21.0 0.8 copy-done.7
  21.8 7.2 %collective-permute-start.1 = (bf16[256,1024]{1,0:T(8,128)(2,1)}, bf16[256,1024]{1,0:T(8,128)(2,1)}, u32[]{:S(2)}, u32[]{:S(2)}) collective-permute-start(bf16[256,1024]{1,0:T(8,128)(2,1)} %get-tuple-element.12), channel_id=1, source_target_pairs={{0,256},{8,264},{16,272},{24,280},{32,288},{40,296},{48,304},{56,3... | collective-permute-start | bytes 1572872 | tf_op jit(solution)/shard_map/ppermute | solution.py:19
  29.1 2.2 %collective-permute-start.2 = (bf16[256,1024]{1,0:T(8,128)(2,1)}, bf16[256,1024]{1,0:T(8,128)(2,1)}, u32[]{:S(2)}, u32[]{:S(2)}) collective-permute-start(bf16[256,1024]{1,0:T(8,128)(2,1)} %get-tuple-element.13), channel_id=1, source_target_pairs={{0,384},{8,392},{16,400},{24,408},{32,416},{40,424},{48,432},{56,4... | collective-permute-start | bytes 1572872 | tf_op jit(solution)/shard_map/ppermute | solution.py:19
  31.3 4.0 %collective-permute-start = (bf16[256,1024]{1,0:T(8,128)(2,1)}, bf16[256,1024]{1,0:T(8,128)(2,1)}, u32[]{:S(2)}, u32[]{:S(2)}) collective-permute-start(bf16[256,1024]{1,0:T(8,128)(2,1)} %get-tuple-element.11), channel_id=1, source_target_pairs={{0,128},{8,136},{16,144},{24,152},{32,160},{40,168},{48,176},{56,1... | collective-permute-start | bytes 1572872 | tf_op jit(solution)/shard_map/ppermute | solution.py:19
  35.3 0.0 copy-done.9
  35.3 0.0 copy-done.10
  35.3 0.0 all-to-all-done
  35.4 10.6 %collective-permute-start.4 = (bf16[8,24,512]{2,1,0:T(8,128)(2,1)S(1)}, bf16[8,24,512]{2,1,0:T(8,128)(2,1)S(1)}, u32[]{:S(2)}, u32[]{:S(2)}) collective-permute-start(bf16[8,24,512]{2,1,0:T(8,128)(2,1)S(1)} %all-to-all-done), channel_id=1, source_target_pairs={{0,40},{8,48},{16,56},{24,0},{32,8},{40,16},{48,24},{56,32},{64,10... | collective-permute-start | bytes 589832 | tf_op jit(solution)/shard_map/ppermute | solution.py:31
  46.0 1.9 %collective-permute-start.3 = (bf16[8,24,512]{2,1,0:T(8,128)(2,1)S(1)}, bf16[8,24,512]{2,1,0:T(8,128)(2,1)S(1)}, u32[]{:S(2)}, u32[]{:S(2)}) collective-permute-start(bf16[8,24,512]{2,1,0:T(8,128)(2,1)S(1)} %all-to-all-done), channel_id=1, source_target_pairs={{0,24},{8,32},{16,40},{24,48},{32,56},{40,0},{48,8},{56,16},{64,88... | collective-permute-start | bytes 589832 | tf_op jit(solution)/shard_map/ppermute | solution.py:31
  48.0 9.6 %collective-permute-done.4 = bf16[8,24,512]{2,1,0:T(8,128)(2,1)S(1)} collective-permute-done((bf16[8,24,512]{2,1,0:T(8,128)(2,1)S(1)}, bf16[8,24,512]{2,1,0:T(8,128)(2,1)S(1)}, u32[]{:S(2)}, u32[]{:S(2)}) %collective-permute-start.4) | collective-permute-done | bytes 196640 | tf_op jit(solution)/shard_map/ppermute | solution.py:31
  57.6 2.5 %collective-permute-start.5 = (bf16[2,8,24,512]{3,2,1,0:T(8,128)(2,1)S(1)}, bf16[2,8,24,512]{3,2,1,0:T(8,128)(2,1)S(1)}, u32[]{:S(2)}, u32[]{:S(2)}) collective-permute-start(bf16[2,8,24,512]{3,2,1,0:T(8,128)(2,1)S(1)} %pad_maximum_fusion.1), channel_id=1, source_target_pairs={{0,8},{8,16},{16,24},{24,32},{32,40},{40,48},{48,56},{56,0},{64,72... | collective-permute-start | bytes 1179656 | tf_op jit(solution)/shard_map/ppermute | solution.py:31
  60.1 4.9 %collective-permute-done.3 = bf16[8,24,512]{2,1,0:T(8,128)(2,1)S(1)} collective-permute-done((bf16[8,24,512]{2,1,0:T(8,128)(2,1)S(1)}, bf16[8,24,512]{2,1,0:T(8,128)(2,1)S(1)}, u32[]{:S(2)}, u32[]{:S(2)}) %collective-permute-start.3) | collective-permute-done | bytes 196640 | tf_op jit(solution)/shard_map/ppermute | solution.py:31
  65.0 0.1 pad_maximum_fusion
  65.1 0.0 copy-start.8
  65.1 2.1 %collective-permute-start.6 = (bf16[3,8,24,512]{3,2,1,0:T(8,128)(2,1)S(1)}, bf16[3,8,24,512]{3,2,1,0:T(8,128)(2,1)S(1)}, u32[]{:S(2)}, u32[]{:S(2)}) collective-permute-start(bf16[3,8,24,512]{3,2,1,0:T(8,128)(2,1)S(1)} %pad_maximum_fusion), channel_id=1, source_target_pairs={{0,56},{8,0},{16,8},{24,16},{32,24},{40,32},{48,40},{56,48},{64,12... | collective-permute-start | bytes 1769480 | tf_op jit(solution)/shard_map/ppermute | solution.py:31
  67.2 6.8 %collective-permute-done.5 = bf16[2,8,24,512]{3,2,1,0:T(8,128)(2,1)S(1)} collective-permute-done((bf16[2,8,24,512]{3,2,1,0:T(8,128)(2,1)S(1)}, bf16[2,8,24,512]{3,2,1,0:T(8,128)(2,1)S(1)}, u32[]{:S(2)}, u32[]{:S(2)}) %collective-permute-start.5) | collective-permute-done | bytes 393248 | tf_op jit(solution)/shard_map/ppermute | solution.py:31
  74.1 7.1 %collective-permute-done.6 = bf16[3,8,24,512]{3,2,1,0:T(8,128)(2,1)S(1)} collective-permute-done((bf16[3,8,24,512]{3,2,1,0:T(8,128)(2,1)S(1)}, bf16[3,8,24,512]{3,2,1,0:T(8,128)(2,1)S(1)}, u32[]{:S(2)}, u32[]{:S(2)}) %collective-permute-start.6) | collective-permute-done | bytes 589856 | tf_op jit(solution)/shard_map/ppermute | solution.py:31
  81.2 3.6 %collective-permute-start.7 = (bf16[8,8,24,512]{3,2,1,0:T(8,128)(2,1)S(1)}, bf16[8,8,24,512]{3,2,1,0:T(8,128)(2,1)S(1)}, u32[]{:S(2)}, u32[]{:S(2)}) collective-permute-start(bf16[8,8,24,512]{3,2,1,0:T(8,128)(2,1)S(1)} %constant_dynamic-update-slice_fusion.mine_ref), channel_id=1, source_target_pairs={{0,1},{1,0},{2,3},{3,2},{4,5},{5,4},{6,7},{7,6},{8,9},{9,8},{10,11... | collective-permute-start | bytes 4718600 | tf_op jit(solution)/shard_map/ppermute | solution.py:24
  84.8 0.0 collective-permute-done.1.refs_2_
  84.8 0.0 collective-permute-done.2.refs_3_
  84.8 0.0 collective-permute-done.refs_1_
  84.8 0.0 copy-done.8
  84.8 0.0 copy-start.3
  84.9 2.9 %pack.1.xs_ref = bf16[560,1536]{1,0:T(8,128)(2,1)S(1)} custom-call(s32[2]{0:T(128)S(1)} %pad_add_fusion.place_ref, s32[4,64]{1,0:T(4,128)S(1)} %bitcast.16, s32[4,64]{1,0:T(4,128)S(1)} %bitcast.19, bf16[256,1024]{1,0:T(8,128)(2,1)S(1)} %copy-done.8, bf16[256,1024]{1,0:T(8,128)(2,1)} %collective-permute-done.refs_1_, ...), custom_call_target="tpu_custom_call" | custom-call | flops 60000002048 | bytes 160000000 | tf_op jit(solution)/shard_map/pack/pallas_call | solution.py:336
  87.8 0.0 copy-start.6
  87.8 1.2 %copy-done.6 = bf16[560,1536]{1,0:T(8,128)(2,1)} copy-done((bf16[560,1536]{1,0:T(8,128)(2,1)}, bf16[560,1536]{1,0:T(8,128)(2,1)S(1)}, u32[]{:S(2)}) %copy-start.6) | copy-done | bytes 1720344
  89.0 0.0 collective-permute-done.7.other_ref
  89.0 0.0 all-gather.2.cloned.1.call-done.weight_ref
  89.0 0.0 copy-done.3
  89.0 20.0 %mix.1 = bf16[512,1536]{1,0:T(8,128)(2,1)} custom-call(s32[2]{0:T(128)S(1)} %pad_add_fusion.place_ref, s32[4,64]{1,0:T(4,128)S(1)} %bitcast.17, s32[4,64]{1,0:T(4,128)S(1)} %bitcast.20, bf16[560,1536]{1,0:T(8,128)(2,1)} %copy-done.6, bf16[8,8,24,512]{3,2,1,0:T(8,128)(2,1)S(1)} %constant_dynamic-update-slice_fusion.mine_ref, ...), custom_call_target="tpu_custom_call" | custom-call | flops 6000000000 | bytes 14000000 | tf_op jit(solution)/shard_map/mix/pallas_call | solution.py:347
  (8 shorter events, 0.2 us)
Async XLA Ops:
  6.5 11.2 %copy-start.5 = (s32[1,64,4]{1,2,0:T(4,128)S(1)}, s32[1,64,4]{1,2,0:T(4,128)}, u32[]{:S(2)}) copy-start(s32[1,64,4]{1,2,0:T(4,128)} %param.11) | copy-start | bytes 3076
  6.5 11.2 %copy-start.4 = (s32[1,64,4]{1,2,0:T(4,128)S(1)}, s32[1,64,4]{1,2,0:T(4,128)}, u32[]{:S(2)}) copy-start(s32[1,64,4]{1,2,0:T(4,128)} %param.10) | copy-start | bytes 3076
  6.5 11.2 %copy-start.2 = (bf16[1024,512]{1,0:T(8,128)(2,1)S(1)}, bf16[1024,512]{1,0:T(8,128)(2,1)}, u32[]{:S(2)}) copy-start(bf16[1024,512]{1,0:T(8,128)(2,1)} %frames_ref.1) | copy-start | bytes 3145732
  6.5 82.4 %all-gather.2.cloned.1.call-start = ((), (), s32[]{:S(2)}) async-start(), calls=%async_computation.1 | async-start | bytes 10616832 | tf_op jit(solution)/shard_map/all_gather | solution.py:301
  7.3 0.7 copy-start
  8.1 0.7 copy-start.1
  10.1 25.3 %all-to-all-start = ((bf16[8,24,512]{2,1,0:T(8,128)(2,1)}), bf16[8,24,512]{2,1,0:T(8,128)(2,1)S(1)}, u32[]{:S(2)}, u32[]{:S(2)}) async-start(bf16[8,24,512]{2,1,0:T(8,128)(2,1)} %own.1), calls=%async_computation | async-start | bytes 393216 | tf_op jit(solution)/shard_map/all_to_all | solution.py:327
  17.7 17.5 %copy-start.9 = (f32[1536]{0:T(1024)S(1)}, f32[1536]{0:T(1024)}, u32[]{:S(2)}) copy-start(f32[1536]{0:T(1024)} %param.16) | copy-start | bytes 18436
  17.8 17.6 %copy-start.10 = (f32[1536]{0:T(1024)S(1)}, f32[1536]{0:T(1024)}, u32[]{:S(2)}) copy-start(f32[1536]{0:T(1024)} %param.17) | copy-start | bytes 18436
  21.0 0.8 copy-start.7
  21.8 63.0 %collective-permute-start.1 = (bf16[256,1024]{1,0:T(8,128)(2,1)}, bf16[256,1024]{1,0:T(8,128)(2,1)}, u32[]{:S(2)}, u32[]{:S(2)}) collective-permute-start(bf16[256,1024]{1,0:T(8,128)(2,1)} %get-tuple-element.12), channel_id=1, source_target_pairs={{0,256},{8,264},{16,272},{24,280},{32,288},{40,296},{48,304},{56,3... | collective-permute-start | bytes 1572872 | tf_op jit(solution)/shard_map/ppermute | solution.py:19
  29.1 55.7 %collective-permute-start.2 = (bf16[256,1024]{1,0:T(8,128)(2,1)}, bf16[256,1024]{1,0:T(8,128)(2,1)}, u32[]{:S(2)}, u32[]{:S(2)}) collective-permute-start(bf16[256,1024]{1,0:T(8,128)(2,1)} %get-tuple-element.13), channel_id=1, source_target_pairs={{0,384},{8,392},{16,400},{24,408},{32,416},{40,424},{48,432},{56,4... | collective-permute-start | bytes 1572872 | tf_op jit(solution)/shard_map/ppermute | solution.py:19
  31.3 53.5 %collective-permute-start = (bf16[256,1024]{1,0:T(8,128)(2,1)}, bf16[256,1024]{1,0:T(8,128)(2,1)}, u32[]{:S(2)}, u32[]{:S(2)}) collective-permute-start(bf16[256,1024]{1,0:T(8,128)(2,1)} %get-tuple-element.11), channel_id=1, source_target_pairs={{0,128},{8,136},{16,144},{24,152},{32,160},{40,168},{48,176},{56,1... | collective-permute-start | bytes 1572872 | tf_op jit(solution)/shard_map/ppermute | solution.py:19
  35.4 22.2 %collective-permute-start.4 = (bf16[8,24,512]{2,1,0:T(8,128)(2,1)S(1)}, bf16[8,24,512]{2,1,0:T(8,128)(2,1)S(1)}, u32[]{:S(2)}, u32[]{:S(2)}) collective-permute-start(bf16[8,24,512]{2,1,0:T(8,128)(2,1)S(1)} %all-to-all-done), channel_id=1, source_target_pairs={{0,40},{8,48},{16,56},{24,0},{32,8},{40,16},{48,24},{56,32},{64,10... | collective-permute-start | bytes 589832 | tf_op jit(solution)/shard_map/ppermute | solution.py:31
  46.0 19.0 %collective-permute-start.3 = (bf16[8,24,512]{2,1,0:T(8,128)(2,1)S(1)}, bf16[8,24,512]{2,1,0:T(8,128)(2,1)S(1)}, u32[]{:S(2)}, u32[]{:S(2)}) collective-permute-start(bf16[8,24,512]{2,1,0:T(8,128)(2,1)S(1)} %all-to-all-done), channel_id=1, source_target_pairs={{0,24},{8,32},{16,40},{24,48},{32,56},{40,0},{48,8},{56,16},{64,88... | collective-permute-start | bytes 589832 | tf_op jit(solution)/shard_map/ppermute | solution.py:31
  57.6 16.4 %collective-permute-start.5 = (bf16[2,8,24,512]{3,2,1,0:T(8,128)(2,1)S(1)}, bf16[2,8,24,512]{3,2,1,0:T(8,128)(2,1)S(1)}, u32[]{:S(2)}, u32[]{:S(2)}) collective-permute-start(bf16[2,8,24,512]{3,2,1,0:T(8,128)(2,1)S(1)} %pad_maximum_fusion.1), channel_id=1, source_target_pairs={{0,8},{8,16},{16,24},{24,32},{32,40},{40,48},{48,56},{56,0},{64,72... | collective-permute-start | bytes 1179656 | tf_op jit(solution)/shard_map/ppermute | solution.py:31
  65.1 19.8 %copy-start.8 = (bf16[256,1024]{1,0:T(8,128)(2,1)S(1)}, bf16[256,1024]{1,0:T(8,128)(2,1)}, u32[]{:S(2)}) copy-start(bf16[256,1024]{1,0:T(8,128)(2,1)} %copy-done.7) | copy-start | bytes 1572868
  65.1 16.0 %collective-permute-start.6 = (bf16[3,8,24,512]{3,2,1,0:T(8,128)(2,1)S(1)}, bf16[3,8,24,512]{3,2,1,0:T(8,128)(2,1)S(1)}, u32[]{:S(2)}, u32[]{:S(2)}) collective-permute-start(bf16[3,8,24,512]{3,2,1,0:T(8,128)(2,1)S(1)} %pad_maximum_fusion), channel_id=1, source_target_pairs={{0,56},{8,0},{16,8},{24,16},{32,24},{40,32},{48,40},{56,48},{64,12... | collective-permute-start | bytes 1769480 | tf_op jit(solution)/shard_map/ppermute | solution.py:31
  81.2 7.8 %collective-permute-start.7 = (bf16[8,8,24,512]{3,2,1,0:T(8,128)(2,1)S(1)}, bf16[8,8,24,512]{3,2,1,0:T(8,128)(2,1)S(1)}, u32[]{:S(2)}, u32[]{:S(2)}) collective-permute-start(bf16[8,8,24,512]{3,2,1,0:T(8,128)(2,1)S(1)} %constant_dynamic-update-slice_fusion.mine_ref), channel_id=1, source_target_pairs={{0,1},{1,0},{2,3},{3,2},{4,5},{5,4},{6,7},{7,6},{8,9},{9,8},{10,11... | collective-permute-start | bytes 4718600 | tf_op jit(solution)/shard_map/ppermute | solution.py:24
  84.8 4.1 %copy-start.3 = (f32[31,1536]{1,0:T(8,128)S(1)}, f32[31,1536]{1,0:T(8,128)}, u32[]{:S(2)}) copy-start(f32[31,1536]{1,0:T(8,128)} %depth_ref.1) | copy-start | bytes 571396
  87.8 1.2 %copy-start.6 = (bf16[560,1536]{1,0:T(8,128)(2,1)}, bf16[560,1536]{1,0:T(8,128)(2,1)S(1)}, u32[]{:S(2)}) copy-start(bf16[560,1536]{1,0:T(8,128)(2,1)S(1)} %pack.1.xs_ref) | copy-start | bytes 5160964
Sparse Core Ops, SparseCore 0:
  9.5 65.3 all-gather.1

commit v5 on v4

--- a/solution.py
+++ b/solution.py
@@ -168,7 +168,7 @@
     lines = mixed_ref.shape[0] // SUBLANES
     lanes = slice(lane, lane + 128)
     weights = [depth_ref[tap : tap + 1, at : at + 128] for tap in range(taps)]
-    span = 10
+    span = 7
     for line in range(0, lines, span):
         near = gated_ref[line : line + span + taps - 1, :, lanes]
         total = near[:span] * weights[0]

time: 116 us -> 117 us (level)
  no operation moved by 1% of the time
where the time goes in v5:
time: 117 us; the launch traced here: 116 us
  starting transfers between devices  41.8 us (36%)
  waiting for transfers between devices  29.1 us (25%)
  Pallas kernels  27.5 us (24%)
  between operations  13.7 us (12%)
  local copies, waits for them, and re-layouts  3.63 us (3%)
    ppermute x4, waiting for transfers between devices, along_z(): return lax.ppermute(value, 'dp', pairs)  28.4 us
    pallas_call x1, Pallas kernels, body(): pl.pallas_call(functools.partial(mix_kernel, node_count, offsets), out_sh...  20.1 us
    ppermute x4, starting transfers between devices, along_z(): return lax.ppermute(value, 'dp', pairs)  17.1 us
    ppermute x3, starting transfers between devices, shifted(): return lax.ppermute(value, axis, pairs)  13.4 us
    all_to_all x1, starting transfers between devices, body(): by_y = lax.all_to_all(copies, 'dp', 0, 0, axis_index_groups=y_groups)  7.65 us
    ppermute x1, starting transfers between devices, core_swapped(): return lax.ppermute(value, axis, [(j, j ^ 1) for j in range(count)])  3.63 us
    unnamed x26, local copies, waits for them, and re-layouts  3.58 us
    pallas_call x1, Pallas kernels, body(): pl.pallas_call(functools.partial(cut_kernel, node_count), out_shape=[jax....  3.27 us
  transfers between devices with their start and end apart: 10, of which 4 were waited for; matrix products, arithmetic and copies ran while one was open for 0% of the time, Pallas kernels for 6%

profile of v5, /device:TPU:1, one launch (start us, length us, event | category | flops | bytes accessed | tf_op | source)
XLA Modules:
  0.0 116.0 jit_solution(6853191274369971559)
XLA Ops:
  6.5 0.0 copy-start.5
  6.5 0.0 copy-start.4
  6.5 0.0 copy-start.2
  6.5 0.0 all-gather.2.cloned.1.call-start
  6.5 0.7 all-gather.2.cloned.1.call-update
  7.3 0.1 pad_add_fusion.place_ref
  7.3 0.0 copy-start
  7.3 0.7 copy-done
  8.1 0.0 copy-start.1
  8.1 0.7 copy-done.1
  8.8 1.3 %own.1 = bf16[8,24,512]{2,1,0:T(8,128)(2,1)} custom-call(s32[2]{0:T(128)S(1)} %pad_add_fusion.place_ref, bf16[24,512]{1,0:T(8,128)(2,1)S(1)} %copy-done, bf16[8,1536]{1,0:T(8,128)(2,1)S(1)} %copy-done.1), custom_call_target="tpu_custom_call" | custom-call | flops 100000 | bytes 300000 | tf_op jit(solution)/shard_map/own/pallas_call | solution.py:318
  10.1 7.7 %all-to-all-start = ((bf16[8,24,512]{2,1,0:T(8,128)(2,1)}), bf16[8,24,512]{2,1,0:T(8,128)(2,1)S(1)}, u32[]{:S(2)}, u32[]{:S(2)}) async-start(bf16[8,24,512]{2,1,0:T(8,128)(2,1)} %own.1), calls=%async_computation | async-start | bytes 393216 | tf_op jit(solution)/shard_map/all_to_all | solution.py:327
  17.7 0.0 copy-done.5
  17.7 0.0 copy-done.4
  17.7 0.0 copy-done.2
  17.7 0.0 copy-start.9
  17.8 0.0 copy-start.10
  17.8 3.3 %cut.1 = (bf16[256,1024]{1,0:T(8,128)(2,1)S(1)}, bf16[256,1024]{1,0:T(8,128)(2,1)}, bf16[256,1024]{1,0:T(8,128)(2,1)}, bf16[256,1024]{1,0:T(8,128)(2,1)}) custom-call(s32[2]{0:T(128)S(1)} %pad_add_fusion.place_ref, s32[4,64]{1,0:T(4,128)S(1)} %bitcast.15, s32[4,64]{1,0:T(4,128)S(1)} %bitcast.18, bf16[1024,512]{1,0:T(8,128)(2,1)S(1)} %copy-done.2), custom_call_target="tpu_custom_call" | custom-call | flops 4000000000 | bytes 4000000 | tf_op jit(solution)/shard_map/cut/pallas_call | solution.py:303
  21.0 0.0 copy-start.7
  21.0 0.8 copy-done.7
  21.8 7.2 %collective-permute-start.1 = (bf16[256,1024]{1,0:T(8,128)(2,1)}, bf16[256,1024]{1,0:T(8,128)(2,1)}, u32[]{:S(2)}, u32[]{:S(2)}) collective-permute-start(bf16[256,1024]{1,0:T(8,128)(2,1)} %get-tuple-element.12), channel_id=1, source_target_pairs={{0,256},{8,264},{16,272},{24,280},{32,288},{40,296},{48,304},{56,3... | collective-permute-start | bytes 1572872 | tf_op jit(solution)/shard_map/ppermute | solution.py:19
  29.1 2.2 %collective-permute-start.2 = (bf16[256,1024]{1,0:T(8,128)(2,1)}, bf16[256,1024]{1,0:T(8,128)(2,1)}, u32[]{:S(2)}, u32[]{:S(2)}) collective-permute-start(bf16[256,1024]{1,0:T(8,128)(2,1)} %get-tuple-element.13), channel_id=1, source_target_pairs={{0,384},{8,392},{16,400},{24,408},{32,416},{40,424},{48,432},{56,4... | collective-permute-start | bytes 1572872 | tf_op jit(solution)/shard_map/ppermute | solution.py:19
  31.3 4.0 %collective-permute-start = (bf16[256,1024]{1,0:T(8,128)(2,1)}, bf16[256,1024]{1,0:T(8,128)(2,1)}, u32[]{:S(2)}, u32[]{:S(2)}) collective-permute-start(bf16[256,1024]{1,0:T(8,128)(2,1)} %get-tuple-element.11), channel_id=1, source_target_pairs={{0,128},{8,136},{16,144},{24,152},{32,160},{40,168},{48,176},{56,1... | collective-permute-start | bytes 1572872 | tf_op jit(solution)/shard_map/ppermute | solution.py:19
  35.3 0.0 copy-done.9
  35.3 0.0 copy-done.10
  35.3 0.0 all-to-all-done
  35.4 10.6 %collective-permute-start.4 = (bf16[8,24,512]{2,1,0:T(8,128)(2,1)S(1)}, bf16[8,24,512]{2,1,0:T(8,128)(2,1)S(1)}, u32[]{:S(2)}, u32[]{:S(2)}) collective-permute-start(bf16[8,24,512]{2,1,0:T(8,128)(2,1)S(1)} %all-to-all-done), channel_id=1, source_target_pairs={{0,40},{8,48},{16,56},{24,0},{32,8},{40,16},{48,24},{56,32},{64,10... | collective-permute-start | bytes 589832 | tf_op jit(solution)/shard_map/ppermute | solution.py:31
  46.0 1.9 %collective-permute-start.3 = (bf16[8,24,512]{2,1,0:T(8,128)(2,1)S(1)}, bf16[8,24,512]{2,1,0:T(8,128)(2,1)S(1)}, u32[]{:S(2)}, u32[]{:S(2)}) collective-permute-start(bf16[8,24,512]{2,1,0:T(8,128)(2,1)S(1)} %all-to-all-done), channel_id=1, source_target_pairs={{0,24},{8,32},{16,40},{24,48},{32,56},{40,0},{48,8},{56,16},{64,88... | collective-permute-start | bytes 589832 | tf_op jit(solution)/shard_map/ppermute | solution.py:31
  48.0 9.6 %collective-permute-done.4 = bf16[8,24,512]{2,1,0:T(8,128)(2,1)S(1)} collective-permute-done((bf16[8,24,512]{2,1,0:T(8,128)(2,1)S(1)}, bf16[8,24,512]{2,1,0:T(8,128)(2,1)S(1)}, u32[]{:S(2)}, u32[]{:S(2)}) %collective-permute-start.4) | collective-permute-done | bytes 196640 | tf_op jit(solution)/shard_map/ppermute | solution.py:31
  57.6 2.5 %collective-permute-start.5 = (bf16[2,8,24,512]{3,2,1,0:T(8,128)(2,1)S(1)}, bf16[2,8,24,512]{3,2,1,0:T(8,128)(2,1)S(1)}, u32[]{:S(2)}, u32[]{:S(2)}) collective-permute-start(bf16[2,8,24,512]{3,2,1,0:T(8,128)(2,1)S(1)} %pad_maximum_fusion.1), channel_id=1, source_target_pairs={{0,8},{8,16},{16,24},{24,32},{32,40},{40,48},{48,56},{56,0},{64,72... | collective-permute-start | bytes 1179656 | tf_op jit(solution)/shard_map/ppermute | solution.py:31
  60.1 4.9 %collective-permute-done.3 = bf16[8,24,512]{2,1,0:T(8,128)(2,1)S(1)} collective-permute-done((bf16[8,24,512]{2,1,0:T(8,128)(2,1)S(1)}, bf16[8,24,512]{2,1,0:T(8,128)(2,1)S(1)}, u32[]{:S(2)}, u32[]{:S(2)}) %collective-permute-start.3) | collective-permute-done | bytes 196640 | tf_op jit(solution)/shard_map/ppermute | solution.py:31
  65.0 0.1 pad_maximum_fusion
  65.1 0.0 copy-start.8
  65.1 2.1 %collective-permute-start.6 = (bf16[3,8,24,512]{3,2,1,0:T(8,128)(2,1)S(1)}, bf16[3,8,24,512]{3,2,1,0:T(8,128)(2,1)S(1)}, u32[]{:S(2)}, u32[]{:S(2)}) collective-permute-start(bf16[3,8,24,512]{3,2,1,0:T(8,128)(2,1)S(1)} %pad_maximum_fusion), channel_id=1, source_target_pairs={{0,56},{8,0},{16,8},{24,16},{32,24},{40,32},{48,40},{56,48},{64,12... | collective-permute-start | bytes 1769480 | tf_op jit(solution)/shard_map/ppermute | solution.py:31
  67.2 6.8 %collective-permute-done.5 = bf16[2,8,24,512]{3,2,1,0:T(8,128)(2,1)S(1)} collective-permute-done((bf16[2,8,24,512]{3,2,1,0:T(8,128)(2,1)S(1)}, bf16[2,8,24,512]{3,2,1,0:T(8,128)(2,1)S(1)}, u32[]{:S(2)}, u32[]{:S(2)}) %collective-permute-start.5) | collective-permute-done | bytes 393248 | tf_op jit(solution)/shard_map/ppermute | solution.py:31
  74.1 7.1 %collective-permute-done.6 = bf16[3,8,24,512]{3,2,1,0:T(8,128)(2,1)S(1)} collective-permute-done((bf16[3,8,24,512]{3,2,1,0:T(8,128)(2,1)S(1)}, bf16[3,8,24,512]{3,2,1,0:T(8,128)(2,1)S(1)}, u32[]{:S(2)}, u32[]{:S(2)}) %collective-permute-start.6) | collective-permute-done | bytes 589856 | tf_op jit(solution)/shard_map/ppermute | solution.py:31
  81.2 3.6 %collective-permute-start.7 = (bf16[8,8,24,512]{3,2,1,0:T(8,128)(2,1)S(1)}, bf16[8,8,24,512]{3,2,1,0:T(8,128)(2,1)S(1)}, u32[]{:S(2)}, u32[]{:S(2)}) collective-permute-start(bf16[8,8,24,512]{3,2,1,0:T(8,128)(2,1)S(1)} %constant_dynamic-update-slice_fusion.mine_ref), channel_id=1, source_target_pairs={{0,1},{1,0},{2,3},{3,2},{4,5},{5,4},{6,7},{7,6},{8,9},{9,8},{10,11... | collective-permute-start | bytes 4718600 | tf_op jit(solution)/shard_map/ppermute | solution.py:24
  84.8 0.0 collective-permute-done.1.refs_2_
  84.8 0.0 collective-permute-done.2.refs_3_
  84.8 0.0 collective-permute-done.refs_1_
  84.8 0.0 copy-done.8
  84.8 0.0 copy-start.3
  84.9 2.9 %pack.1.xs_ref = bf16[560,1536]{1,0:T(8,128)(2,1)S(1)} custom-call(s32[2]{0:T(128)S(1)} %pad_add_fusion.place_ref, s32[4,64]{1,0:T(4,128)S(1)} %bitcast.16, s32[4,64]{1,0:T(4,128)S(1)} %bitcast.19, bf16[256,1024]{1,0:T(8,128)(2,1)S(1)} %copy-done.8, bf16[256,1024]{1,0:T(8,128)(2,1)} %collective-permute-done.refs_1_, ...), custom_call_target="tpu_custom_call" | custom-call | flops 60000002048 | bytes 160000000 | tf_op jit(solution)/shard_map/pack/pallas_call | solution.py:336
  87.8 0.0 copy-start.6
  87.8 1.2 %copy-done.6 = bf16[560,1536]{1,0:T(8,128)(2,1)} copy-done((bf16[560,1536]{1,0:T(8,128)(2,1)}, bf16[560,1536]{1,0:T(8,128)(2,1)S(1)}, u32[]{:S(2)}) %copy-start.6) | copy-done | bytes 1720344
  89.0 0.0 collective-permute-done.7.other_ref
  89.0 0.0 all-gather.2.cloned.1.call-done.weight_ref
  89.0 0.0 copy-done.3
  89.0 20.1 %mix.1 = bf16[512,1536]{1,0:T(8,128)(2,1)} custom-call(s32[2]{0:T(128)S(1)} %pad_add_fusion.place_ref, s32[4,64]{1,0:T(4,128)S(1)} %bitcast.17, s32[4,64]{1,0:T(4,128)S(1)} %bitcast.20, bf16[560,1536]{1,0:T(8,128)(2,1)} %copy-done.6, bf16[8,8,24,512]{3,2,1,0:T(8,128)(2,1)S(1)} %constant_dynamic-update-slice_fusion.mine_ref, ...), custom_call_target="tpu_custom_call" | custom-call | flops 6000000000 | bytes 14000000 | tf_op jit(solution)/shard_map/mix/pallas_call | solution.py:347
  (8 shorter events, 0.2 us)
Async XLA Ops:
  6.5 11.2 %copy-start.5 = (s32[1,64,4]{1,2,0:T(4,128)S(1)}, s32[1,64,4]{1,2,0:T(4,128)}, u32[]{:S(2)}) copy-start(s32[1,64,4]{1,2,0:T(4,128)} %param.11) | copy-start | bytes 3076
  6.5 11.2 %copy-start.4 = (s32[1,64,4]{1,2,0:T(4,128)S(1)}, s32[1,64,4]{1,2,0:T(4,128)}, u32[]{:S(2)}) copy-start(s32[1,64,4]{1,2,0:T(4,128)} %param.10) | copy-start | bytes 3076
  6.5 11.2 %copy-start.2 = (bf16[1024,512]{1,0:T(8,128)(2,1)S(1)}, bf16[1024,512]{1,0:T(8,128)(2,1)}, u32[]{:S(2)}) copy-start(bf16[1024,512]{1,0:T(8,128)(2,1)} %frames_ref.1) | copy-start | bytes 3145732
  6.5 82.4 %all-gather.2.cloned.1.call-start = ((), (), s32[]{:S(2)}) async-start(), calls=%async_computation.1 | async-start | bytes 10616832 | tf_op jit(solution)/shard_map/all_gather | solution.py:301
  7.3 0.7 copy-start
  8.1 0.7 copy-start.1
  10.1 25.3 %all-to-all-start = ((bf16[8,24,512]{2,1,0:T(8,128)(2,1)}), bf16[8,24,512]{2,1,0:T(8,128)(2,1)S(1)}, u32[]{:S(2)}, u32[]{:S(2)}) async-start(bf16[8,24,512]{2,1,0:T(8,128)(2,1)} %own.1), calls=%async_computation | async-start | bytes 393216 | tf_op jit(solution)/shard_map/all_to_all | solution.py:327
  17.7 17.5 %copy-start.9 = (f32[1536]{0:T(1024)S(1)}, f32[1536]{0:T(1024)}, u32[]{:S(2)}) copy-start(f32[1536]{0:T(1024)} %param.16) | copy-start | bytes 18436
  17.8 17.6 %copy-start.10 = (f32[1536]{0:T(1024)S(1)}, f32[1536]{0:T(1024)}, u32[]{:S(2)}) copy-start(f32[1536]{0:T(1024)} %param.17) | copy-start | bytes 18436
  21.0 0.8 copy-start.7
  21.8 63.0 %collective-permute-start.1 = (bf16[256,1024]{1,0:T(8,128)(2,1)}, bf16[256,1024]{1,0:T(8,128)(2,1)}, u32[]{:S(2)}, u32[]{:S(2)}) collective-permute-start(bf16[256,1024]{1,0:T(8,128)(2,1)} %get-tuple-element.12), channel_id=1, source_target_pairs={{0,256},{8,264},{16,272},{24,280},{32,288},{40,296},{48,304},{56,3... | collective-permute-start | bytes 1572872 | tf_op jit(solution)/shard_map/ppermute | solution.py:19
  29.1 55.7 %collective-permute-start.2 = (bf16[256,1024]{1,0:T(8,128)(2,1)}, bf16[256,1024]{1,0:T(8,128)(2,1)}, u32[]{:S(2)}, u32[]{:S(2)}) collective-permute-start(bf16[256,1024]{1,0:T(8,128)(2,1)} %get-tuple-element.13), channel_id=1, source_target_pairs={{0,384},{8,392},{16,400},{24,408},{32,416},{40,424},{48,432},{56,4... | collective-permute-start | bytes 1572872 | tf_op jit(solution)/shard_map/ppermute | solution.py:19
  31.3 53.5 %collective-permute-start = (bf16[256,1024]{1,0:T(8,128)(2,1)}, bf16[256,1024]{1,0:T(8,128)(2,1)}, u32[]{:S(2)}, u32[]{:S(2)}) collective-permute-start(bf16[256,1024]{1,0:T(8,128)(2,1)} %get-tuple-element.11), channel_id=1, source_target_pairs={{0,128},{8,136},{16,144},{24,152},{32,160},{40,168},{48,176},{56,1... | collective-permute-start | bytes 1572872 | tf_op jit(solution)/shard_map/ppermute | solution.py:19
  35.4 22.2 %collective-permute-start.4 = (bf16[8,24,512]{2,1,0:T(8,128)(2,1)S(1)}, bf16[8,24,512]{2,1,0:T(8,128)(2,1)S(1)}, u32[]{:S(2)}, u32[]{:S(2)}) collective-permute-start(bf16[8,24,512]{2,1,0:T(8,128)(2,1)S(1)} %all-to-all-done), channel_id=1, source_target_pairs={{0,40},{8,48},{16,56},{24,0},{32,8},{40,16},{48,24},{56,32},{64,10... | collective-permute-start | bytes 589832 | tf_op jit(solution)/shard_map/ppermute | solution.py:31
  46.0 19.0 %collective-permute-start.3 = (bf16[8,24,512]{2,1,0:T(8,128)(2,1)S(1)}, bf16[8,24,512]{2,1,0:T(8,128)(2,1)S(1)}, u32[]{:S(2)}, u32[]{:S(2)}) collective-permute-start(bf16[8,24,512]{2,1,0:T(8,128)(2,1)S(1)} %all-to-all-done), channel_id=1, source_target_pairs={{0,24},{8,32},{16,40},{24,48},{32,56},{40,0},{48,8},{56,16},{64,88... | collective-permute-start | bytes 589832 | tf_op jit(solution)/shard_map/ppermute | solution.py:31
  57.6 16.4 %collective-permute-start.5 = (bf16[2,8,24,512]{3,2,1,0:T(8,128)(2,1)S(1)}, bf16[2,8,24,512]{3,2,1,0:T(8,128)(2,1)S(1)}, u32[]{:S(2)}, u32[]{:S(2)}) collective-permute-start(bf16[2,8,24,512]{3,2,1,0:T(8,128)(2,1)S(1)} %pad_maximum_fusion.1), channel_id=1, source_target_pairs={{0,8},{8,16},{16,24},{24,32},{32,40},{40,48},{48,56},{56,0},{64,72... | collective-permute-start | bytes 1179656 | tf_op jit(solution)/shard_map/ppermute | solution.py:31
  65.1 19.8 %copy-start.8 = (bf16[256,1024]{1,0:T(8,128)(2,1)S(1)}, bf16[256,1024]{1,0:T(8,128)(2,1)}, u32[]{:S(2)}) copy-start(bf16[256,1024]{1,0:T(8,128)(2,1)} %copy-done.7) | copy-start | bytes 1572868
  65.1 16.0 %collective-permute-start.6 = (bf16[3,8,24,512]{3,2,1,0:T(8,128)(2,1)S(1)}, bf16[3,8,24,512]{3,2,1,0:T(8,128)(2,1)S(1)}, u32[]{:S(2)}, u32[]{:S(2)}) collective-permute-start(bf16[3,8,24,512]{3,2,1,0:T(8,128)(2,1)S(1)} %pad_maximum_fusion), channel_id=1, source_target_pairs={{0,56},{8,0},{16,8},{24,16},{32,24},{40,32},{48,40},{56,48},{64,12... | collective-permute-start | bytes 1769480 | tf_op jit(solution)/shard_map/ppermute | solution.py:31
  81.2 7.8 %collective-permute-start.7 = (bf16[8,8,24,512]{3,2,1,0:T(8,128)(2,1)S(1)}, bf16[8,8,24,512]{3,2,1,0:T(8,128)(2,1)S(1)}, u32[]{:S(2)}, u32[]{:S(2)}) collective-permute-start(bf16[8,8,24,512]{3,2,1,0:T(8,128)(2,1)S(1)} %constant_dynamic-update-slice_fusion.mine_ref), channel_id=1, source_target_pairs={{0,1},{1,0},{2,3},{3,2},{4,5},{5,4},{6,7},{7,6},{8,9},{9,8},{10,11... | collective-permute-start | bytes 4718600 | tf_op jit(solution)/shard_map/ppermute | solution.py:24
  84.8 4.1 %copy-start.3 = (f32[31,1536]{1,0:T(8,128)S(1)}, f32[31,1536]{1,0:T(8,128)}, u32[]{:S(2)}) copy-start(f32[31,1536]{1,0:T(8,128)} %depth_ref.1) | copy-start | bytes 571396
  87.8 1.2 %copy-start.6 = (bf16[560,1536]{1,0:T(8,128)(2,1)}, bf16[560,1536]{1,0:T(8,128)(2,1)S(1)}, u32[]{:S(2)}) copy-start(bf16[560,1536]{1,0:T(8,128)(2,1)S(1)} %pack.1.xs_ref) | copy-start | bytes 5160964
Sparse Core Ops, SparseCore 0:
  9.5 65.3 all-gather.1
